TPU v7x, 512 devices: a whole 4x8x8 slice. The times are simulated.
512 devices in a mesh: src: 16 (over z_hi, x, core), rows: 32 (over z_lo, y).
Axes of the slice: x: 4, y: 8, z: 8 (z_hi: 2, z_lo: 4; z = z_hi * 4 + z_lo), core: 2. Of those that a mesh axis runs over, the one named last changes fastest.
Arguments:
- mask_param: float32 [512, 8192], P('rows'), may hold values from -6 to 6
- target: int32 [512, 8192], P('rows', 'src'), may hold values 0 or 1
- source_weight: float32 [16], replicated, may hold values from 0.25 to 4
- row_shift: int32 [16], replicated, may hold values from -8 to 8
- col_shift: int32 [16], replicated, may hold values from -32 to 32
Outputs:
- mask_grad: float32 [512, 8192], P('rows', 'src')
All inputs are finite; a program needn't handle non-finite values. No bound on the sum of `target` on one device may be relied on, other than what follows from the above.
Results may differ from a plain program's by a relative error of at most 0.0003.
Values sent between devices are 32-bit elements; how exact they have to be, the bound alone decides.
No kernel may reach another device: no remote copies, remote signals or barrier semaphores. Data moves between devices by JAX's collectives and lax.ppermute only.
A program may use at most 64 MiB of HBM per device.

v0:
```python
import math

import jax
import jax.numpy as jnp
from jax import lax
from jax.sharding import PartitionSpec as P

steepness = 250.0
threshold_level = 0.25
loss_weight = 8.0
highest = lax.Precision.HIGHEST


def product(matrix_left, matrix_right):
    return jnp.dot(matrix_left, matrix_right, precision=highest, preferred_element_type=jnp.float32)


def product_nt(matrix_left, matrix_right):
    return lax.dot_general(
        matrix_left,
        matrix_right,
        (((1,), (1,)), ((), ())),
        precision=highest,
        preferred_element_type=jnp.float32,
    )


def product_tn(matrix_left, matrix_right):
    return lax.dot_general(
        matrix_left,
        matrix_right,
        (((0,), (0,)), ((), ())),
        precision=highest,
        preferred_element_type=jnp.float32,
    )


def centered(number):
    return jnp.arange(number, dtype=jnp.int32) - number // 2


def phases(frequency, position, period):
    angles = jnp.mod(position[:, None] * frequency[None, :], period).astype(jnp.float32) * (
        2.0 * math.pi / period
    )
    return (jnp.cos(angles), jnp.sin(angles))


def pupil_mask(row_offset, col_offset, band_rows, band_cols):
    radius_rows = band_rows // 4
    radius_cols = band_cols // 4
    row_term = (centered(band_rows) + row_offset) ** 2 * (radius_cols * radius_cols)
    col_term = (centered(band_cols) + col_offset) ** 2 * (radius_rows * radius_rows)
    limit_value = (radius_rows * radius_cols) ** 2
    return (row_term[:, None] + col_term[None, :] <= limit_value).astype(jnp.float32)


def columns_forward(real_part, imag_part, column_start, band_cols, total_columns):
    row_count, col_width = real_part.shape
    block_width = min(512, col_width)
    block_count = col_width // block_width
    frequency = centered(band_cols)
    base_cos, base_sin = phases(frequency, jnp.arange(block_width, dtype=jnp.int32), total_columns)
    starts = column_start + block_width * jnp.arange(block_count, dtype=jnp.int32)
    twist_cos, twist_sin = phases(frequency, starts, total_columns)
    stack_rows = row_count * block_count
    if imag_part is None:
        flat_real = real_part.reshape(stack_rows, block_width)
        part_real = product(flat_real, base_cos)
        part_imag = -product(flat_real, base_sin)
    else:
        stacked = jnp.concatenate(
            [
                real_part.reshape(stack_rows, block_width),
                imag_part.reshape(stack_rows, block_width),
            ],
            axis=0,
        )
        with_cos = product(stacked, base_cos)
        with_sin = product(stacked, base_sin)
        part_real = with_cos[:stack_rows] + with_sin[stack_rows:]
        part_imag = with_cos[stack_rows:] - with_sin[:stack_rows]
    part_real = part_real.reshape(row_count, block_count, band_cols)
    part_imag = part_imag.reshape(row_count, block_count, band_cols)
    out_real = jnp.sum(part_real * twist_cos + part_imag * twist_sin, axis=1)
    out_imag = jnp.sum(part_imag * twist_cos - part_real * twist_sin, axis=1)
    return (out_real, out_imag)


def rows_forward(real_part, imag_part, row_start, band_rows, total_rows):
    position = row_start + jnp.arange(real_part.shape[0], dtype=jnp.int32)
    row_cos, row_sin = phases(centered(band_rows), position, total_rows)
    out_real = product_tn(row_cos, real_part) + product_tn(row_sin, imag_part)
    out_imag = product_tn(row_cos, imag_part) - product_tn(row_sin, real_part)
    return (out_real, out_imag)


def rows_inverse(real_part, imag_part, row_start, row_count, total_rows):
    position = row_start + jnp.arange(row_count, dtype=jnp.int32)
    row_cos, row_sin = phases(centered(real_part.shape[0]), position, total_rows)
    out_real = product(row_cos, real_part) - product(row_sin, imag_part)
    out_imag = product(row_cos, imag_part) + product(row_sin, real_part)
    return (out_real, out_imag)


def columns_inverse(real_part, imag_part, column_start, width_out, total_columns):
    row_count, band_cols = real_part.shape
    block_width = min(512, width_out)
    block_count = width_out // block_width
    frequency = centered(band_cols)
    base_cos, base_sin = phases(frequency, jnp.arange(block_width, dtype=jnp.int32), total_columns)
    starts = column_start + block_width * jnp.arange(block_count, dtype=jnp.int32)
    twist_cos, twist_sin = phases(frequency, starts, total_columns)
    turned_real = real_part[:, None, :] * twist_cos - imag_part[:, None, :] * twist_sin
    turned_imag = real_part[:, None, :] * twist_sin + imag_part[:, None, :] * twist_cos
    stack_rows = row_count * block_count
    stacked = jnp.concatenate(
        [turned_real.reshape(stack_rows, band_cols), turned_imag.reshape(stack_rows, band_cols)],
        axis=0,
    )
    with_cos = product_nt(stacked, base_cos)
    with_sin = product_nt(stacked, base_sin)
    field_real = (with_cos[:stack_rows] - with_sin[stack_rows:]).reshape(row_count, width_out)
    field_imag = (with_sin[:stack_rows] + with_cos[stack_rows:]).reshape(row_count, width_out)
    return (field_real, field_imag)


def resist_slope(intensity, target):
    resist = jax.nn.sigmoid(steepness * (intensity - threshold_level))
    return (
        2.0
        * loss_weight
        * (resist - target.astype(jnp.float32))
        * steepness
        * resist
        * (1.0 - resist)
    )


def local(mask_param, target, source_weight, row_shift, col_shift):
    row_block, total_columns = mask_param.shape
    src_count = lax.axis_size("src")
    src_index = lax.axis_index("src")
    row_index = lax.axis_index("rows")
    total_rows = row_block * lax.axis_size("rows")
    band_rows = total_rows // 16
    band_cols = total_columns // 64
    col_share = total_columns // src_count
    local_points = source_weight.shape[0] // src_count
    row_start = row_index * row_block
    share_start = src_index * col_share
    unit_scale = 1.0 / math.sqrt(total_rows * total_columns)
    opening = jax.nn.sigmoid(mask_param)
    all_weights = source_weight / jnp.sum(source_weight)
    col_real, col_imag = columns_forward(opening, None, 0, band_cols, total_columns)
    part_real, part_imag = rows_forward(col_real, col_imag, row_start, band_rows, total_rows)
    band_real, band_imag = lax.psum((part_real * unit_scale, part_imag * unit_scale), "rows")
    my_weights = lax.dynamic_slice_in_dim(all_weights, src_index * local_points, local_points)
    my_rows = lax.dynamic_slice_in_dim(row_shift, src_index * local_points, local_points)
    my_cols = lax.dynamic_slice_in_dim(col_shift, src_index * local_points, local_points)
    source_point = 0
    opened = pupil_mask(my_rows[source_point], my_cols[source_point], band_rows, band_cols)
    head_real, head_imag = rows_inverse(
        band_real * opened * unit_scale,
        band_imag * opened * unit_scale,
        row_start,
        row_block,
        total_rows,
    )
    field_real, field_imag = columns_inverse(head_real, head_imag, 0, total_columns, total_columns)
    intensity_part = my_weights[source_point] * (field_real * field_real + field_imag * field_imag)
    field_list = [(field_real, field_imag)]
    pupil_list = [opened]
    intensity = lax.psum_scatter(intensity_part, "src", scatter_dimension=1, tiled=True)
    slope_share = resist_slope(intensity, target)
    slope = lax.all_gather(slope_share, "src", axis=1, tiled=True)
    source_point = 0
    field_real, field_imag = field_list[source_point]
    factor = 2.0 * my_weights[source_point] * slope
    cot_real, cot_imag = columns_forward(
        factor * field_real, factor * field_imag, 0, band_cols, total_columns
    )
    back_real, back_imag = rows_forward(cot_real, cot_imag, row_start, band_rows, total_rows)
    adjoint_real = pupil_list[source_point] * back_real
    adjoint_imag = pupil_list[source_point] * back_imag
    adjoint_real, adjoint_imag = lax.psum(
        (adjoint_real * unit_scale, adjoint_imag * unit_scale), ("src", "rows")
    )
    head_real, head_imag = rows_inverse(
        adjoint_real * unit_scale, adjoint_imag * unit_scale, row_start, row_block, total_rows
    )
    grad_real, grad_imag = columns_inverse(
        head_real, head_imag, share_start, col_share, total_columns
    )
    own_open = lax.dynamic_slice_in_dim(opening, share_start, col_share, 1)
    return grad_real * own_open * (1.0 - own_open)


def solution(mesh):
    placed = (P("rows", None), P("rows", "src"), P(), P(), P())
    return jax.shard_map(
        local, mesh=mesh, in_specs=placed, out_specs=P("rows", "src"), check_vma=False
    )
```

profile of v0, /device:TPU:6, one launch (start us, length us, event | category | flops | bytes accessed | tf_op | source)
XLA Modules:
  0.0 406.5 jit_solution(5263452524671067689)
XLA Ops:
  6.5 0.0 reduce-scatter.2.cloned.1.call-start
  6.5 1.2 add_divide_fusion
  7.7 0.1 reshape.193
  7.8 0.1 fusion.73
  8.0 1.5 convolution_negate_fusion
  9.5 0.3 copy.6
  9.9 1.5 add_reduce_fusion.1
  11.4 0.3 fusion.86
  11.7 0.3 fusion.83
  12.1 0.3 fusion.7
  12.4 0.3 fusion.6
  12.8 0.0 copy-start.1
  12.8 0.6 copy-done.1
  13.5 0.6 dynamic_slice.13
  14.0 0.0 copy-start.2
  14.0 0.7 multiply_multiply_fusion.2
  14.7 0.0 copy-done.2
  14.7 0.6 dynamic_slice.12
  15.3 0.7 multiply_multiply_fusion.3
  16.0 156.0 %all-reduce.1 = (f32[32,128]{1,0:T(8,128)S(1)}, f32[32,128]{1,0:T(8,128)S(1)}) all-reduce(f32[32,128]{1,0:T(8,128)S(1)} %fusion.6, f32[32,128]{1,0:T(8,128)S(1)} %fusion.7), channel_id=1, replica_groups=mesh['src'=16,'rows'=32] {'rows'}, use_global_device_ids=true, to_apply=%region_4.5 | all-reduce | flops 8192 | bytes 65536 | tf_op jit(solution)/shard_map/psum | solution.py:157
  171.9 0.2 fusion.37
  172.2 0.3 fusion.38
  172.4 0.3 convolution_subtract_fusion.4
  172.7 0.3 convolution_add_fusion.3
  173.0 1.9 fusion.16
  174.9 1.9 fusion.17
  176.9 0.2 slice_add_fusion
  177.1 0.1 reshape.195
  177.2 0.0 copy-start.3
  177.2 0.1 reshape.196
  177.3 0.5 copy-done.3
  177.9 0.6 reduce_sum.45
  178.5 0.6 broadcast_divide_fusion
  179.1 0.6 dynamic_slice.14
  179.7 1.5 add_multiply_fusion
  181.2 0.0 copy-start
  181.2 0.0 reduce-scatter.2.cloned.1.call-update
  181.9 0.1 fusion.123
  181.9 81.3 %reduce-scatter.2.cloned.1.call-done = f32[16,512]{1,0:T(8,128)} async-done(((f32[16,8192]{1,0:T(8,128)}), f32[16,512]{1,0:T(8,128)}) %reduce-scatter.2.cloned.1.call-update) | async-done | bytes 32784 | tf_op jit(solution)/shard_map/reduce_scatter | solution.py:174
  263.3 0.0 copy-done
  263.3 0.8 subtract_multiply_fusion
  264.0 24.7 %all_gather.3 = f32[16,8192]{1,0:T(8,128)S(1)} all-gather(f32[16,512]{1,0:T(8,128)S(1)} %subtract_multiply_fusion), channel_id=1, replica_groups=mesh['src'=16,'rows'=32] {'src'}, dimensions={1}, use_global_device_ids=true | all-gather | bytes 557056 | tf_op jit(solution)/shard_map/all_gather | solution.py:176
  288.7 0.1 multiply_multiply_fusion
  288.8 0.1 reshape.197
  289.0 0.1 reshape.198
  289.1 1.9 fusion.22
  291.0 1.9 fusion.27
  293.0 0.1 add_reduce_fusion
  293.1 0.3 fusion.80
  293.4 0.3 fusion.77
  293.7 0.3 fusion.5
  294.1 0.3 fusion.3
  294.4 100.9 %all-reduce = (f32[32,128]{1,0:T(8,128)S(1)}, f32[32,128]{1,0:T(8,128)S(1)}) all-reduce(f32[32,128]{1,0:T(8,128)S(1)} %fusion.3, f32[32,128]{1,0:T(8,128)S(1)} %fusion.5), channel_id=1, replica_groups=mesh['src'=16,'rows'=32] {'src','rows'}, use_global_device_ids=true, to_apply=%region_9.10 | all-reduce | flops 8192 | bytes 65536 | tf_op jit(solution)/shard_map/psum | solution.py:186
  395.3 0.3 fusion.35
  395.6 0.3 fusion.31
  395.9 0.3 convolution_subtract_fusion.3
  396.1 0.3 multiply_add_fusion.1
  396.4 1.3 fusion.20
  397.7 1.9 fusion.1
  (7 shorter events, 0.1 us)
Async XLA Ops:
  6.5 256.7 %reduce-scatter.2.cloned.1.call-start = ((), (), s32[]{:S(2)}) async-start(), calls=%async_computation.1 | async-start | bytes 557056 | tf_op jit(solution)/shard_map/reduce_scatter | solution.py:174
  12.8 0.7 copy-start.1
  14.0 0.7 copy-start.2
  177.2 0.7 copy-start.3
  181.2 82.0 %copy-start = (s32[16,512]{1,0:T(8,128)S(1)}, s32[16,512]{1,0:T(8,128)}, u32[]{:S(2)}) copy-start(s32[16,512]{1,0:T(8,128)} %param.6) | copy-start | bytes 98308
Sparse Core Ops, SparseCore 0:
  181.4 81.8 reduce-scatter.1
where the time goes:
time: 408 us; the launch traced here: 406 us
  blocking collectives  282 us (69%)
  waiting for transfers between devices  81.3 us (20%)
  matrix products  18.8 us (5%)
  between operations  14.3 us (4%)
  other arithmetic  6.64 us (2%)
    psum x1, blocking collectives, local(): lax.psum((part_real * unit_scale, part_imag * unit_scale), 'rows')  156 us
    psum x1, blocking collectives, local(): lax.psum((adjoint_real * unit_scale, adjoint_imag * unit_scale), ('src',...  101 us
    reduce_scatter x1, waiting for transfers between devices, local(): lax.psum_scatter(intensity_part, 'src', scatter_dimension=1, tiled=True)  81.3 us
    all_gather x1, blocking collectives, local(): slope = lax.all_gather(slope_share, 'src', axis=1, tiled=True)  24.7 us
    dot_general x12, matrix products, product(): jnp.dot(matrix_left, matrix_right, precision=highest, preferred_element_t...  8.98 us
  transfers between devices with their start and end apart: 1, of which 1 were waited for; matrix products, arithmetic and copies ran while one was open for 0% of the time, Pallas kernels for 0%

commit v1 on v0

v1 whole, which is shorter than its diff:
```python
import math

import jax
import jax.numpy as jnp
import numpy as np
from jax import lax
from jax.sharding import PartitionSpec as P

steepness = 250.0
threshold_level = 0.25
loss_weight = 8.0
highest = lax.Precision.HIGHEST

NR = 512
NC = 8192
KR = 32
KC = 128
MC = 256
HALF = KC // 2
SHARE = 512
BLOCKS = NC // SHARE
ROWS = 16
UNIT = 1.0 / math.sqrt(NR * NC)


def dot(left, right, precision=highest):
    return jnp.dot(left, right, precision=precision, preferred_element_type=jnp.float32)


def wave(frequency, position, period):
    angle = (np.outer(frequency, position) % period) * (2.0 * np.pi / period)
    return np.cos(angle), np.sin(angle)


def f32(table):
    return np.asarray(table, dtype=np.float32)


def column_tables():
    half = np.arange(HALF)
    cos, sin = wave(np.arange(HALF + 1), np.arange(SHARE), NC)
    real, imag = cos, -sin
    first = np.concatenate([real[:HALF], real[HALF:], imag[1:HALF]])
    second = np.concatenate([imag[:HALF], imag[HALF:], real[1:HALF]])
    base = np.concatenate([first, second]).T
    order = np.concatenate([half, [HALF], half[1:]])
    sign = np.concatenate([np.ones(HALF + 1), -np.ones(HALF - 1)])
    turn_cos, turn_sin = wave(np.arange(BLOCKS), order, BLOCKS)
    return f32(base), f32(turn_cos), f32(turn_sin * sign), f32(turn_sin)


def spread_table():
    table = np.zeros((KC + 1, 2 * KC))
    for frequency in range(-HALF, HALF):
        size = abs(frequency)
        at = frequency + HALF
        table[size if size < HALF else HALF, at] = 1.0
        if size == HALF:
            table[KC, KC + at] = -1.0
        elif size > 0:
            table[HALF + size, KC + at] = 1.0 if frequency > 0 else -1.0
    return f32(table)


def row_table():
    cos, sin = wave(np.arange(KR) - KR // 2, np.arange(NR), NR)
    return f32(np.concatenate([cos, sin]))


def sample_tables():
    cos, sin = wave(np.arange(KC) - HALF, np.arange(MC), MC)
    inverse = np.block([[cos, sin], [-sin, cos]])
    return f32(inverse), f32(inverse.T)


def interpolation_table():
    size = np.arange(1, HALF + 1)
    place = (np.arange(MC)[:, None] * (NC // MC) - np.arange(SHARE)[None, :]) % NC
    total = np.ones_like(place, dtype=np.float64)
    for k in size:
        total += 2.0 * np.cos(((place * k) % NC) * (2.0 * np.pi / NC))
    return f32(total / MC)


def fold_tables():
    columns = np.zeros((KC, KC + 1))
    odd = np.zeros((KC, KC + 1))
    even = np.zeros((KC, KC + 1))
    for frequency in range(-HALF, HALF):
        at, size = frequency + HALF, abs(frequency)
        even[at, size] = 1.0
        if size > 0:
            odd[at, size - 1] = -1.0 if frequency > 0 else 1.0
    columns = np.concatenate([even[:, : HALF + 1], odd[:, :HALF]], axis=1)
    rows_even = np.zeros((KR // 2 + 1, KR))
    rows_odd = np.zeros((KR // 2 + 1, KR))
    for frequency in range(-KR // 2, KR // 2):
        at, size = frequency + KR // 2, abs(frequency)
        rows_even[size, at] = 1.0
        rows_odd[size, at] = float(np.sign(frequency))
    return f32(columns), f32(rows_even), f32(rows_odd)


def final_tables():
    cos, sin = wave(np.arange(NR), np.arange(KR // 2 + 1), NR)
    rows = np.concatenate([cos, sin], axis=1)
    cos_y, sin_y = wave(np.arange(HALF + 1), np.arange(SHARE), NC)
    columns = np.concatenate([cos_y, sin_y[1:]])
    turn_cos, turn_sin = wave(np.arange(BLOCKS), np.arange(HALF + 1), BLOCKS)
    return f32(rows), f32(columns), f32(turn_cos), f32(turn_sin)


def everywhere(values, axis, count):
    spread = jnp.broadcast_to(values[None], (count,) + values.shape)
    return lax.all_to_all(spread, axis, 0, 0, tiled=True)


def pupils(row_shift, col_shift):
    radius_rows = KR // 4
    radius_cols = KC // 4
    fr = jnp.arange(KR, dtype=jnp.int32) - KR // 2
    fc = jnp.arange(KC, dtype=jnp.int32) - HALF
    row_term = (fr[:, None] + row_shift[None, :]) ** 2 * (radius_cols * radius_cols)
    col_term = (fc[None, :] + col_shift[:, None]) ** 2 * (radius_rows * radius_rows)
    limit_value = (radius_rows * radius_cols) ** 2
    return (row_term[:, :, None] + col_term[None] <= limit_value).astype(jnp.float32)


def local(mask_param, target, source_weight, row_shift, col_shift):
    src_index = lax.axis_index("src")
    row_index = lax.axis_index("rows")
    src_count = lax.axis_size("src")
    row_count = lax.axis_size("rows")
    points = source_weight.shape[0]
    opening = jax.nn.sigmoid(mask_param)
    weights = source_weight / jnp.sum(source_weight)
    opened = pupils(row_shift, col_shift)

    base, turn_cos, turn_side, turn_sin = column_tables()
    stacked = jnp.concatenate([opening[:, SHARE * b : SHARE * (b + 1)] for b in range(BLOCKS)])
    parts = dot(stacked, base).reshape(BLOCKS, ROWS, 2 * KC)
    first, second = parts[:, :, :KC], parts[:, :, KC:]
    packed = jnp.sum(first * turn_cos[:, None] + second * turn_side[:, None], axis=0)
    edge = jnp.sum(
        second[:, :, HALF] * turn_cos[:, None, HALF] - first[:, :, HALF] * turn_sin[:, None, HALF],
        axis=0,
    )
    message = jnp.concatenate([packed, jnp.pad(edge, (0, KC - ROWS))[None]])
    heard = everywhere(message, "rows", row_count)
    column_part = jnp.concatenate(
        [heard[:, :ROWS].reshape(NR, KC), heard[:, ROWS, :ROWS].reshape(NR, 1)], axis=1
    )
    both = dot(dot(row_table() * UNIT, column_part), spread_table())
    cr, ci = both[:KR, :KC], both[:KR, KC:]
    sr, si = both[KR:, :KC], both[KR:, KC:]
    band_real, band_imag = cr + si, ci - sr

    own = lax.dynamic_slice_in_dim(jnp.asarray(row_table().T), row_index * ROWS, ROWS)
    own_cos, own_sin = own[:, :KR], own[:, KR:]
    turn = jnp.concatenate(
        [
            jnp.concatenate([own_cos, -own_sin], axis=1),
            jnp.concatenate([own_sin, own_cos], axis=1),
        ]
    )
    masked = jnp.concatenate([band_real[:, None] * opened, band_imag[:, None] * opened])
    head = dot(turn * UNIT, masked.reshape(2 * KR, points * KC)).reshape(2, ROWS, points, KC)
    head = head.transpose(2, 1, 0, 3).reshape(points * ROWS, 2 * KC)
    to_samples, from_samples = sample_tables()
    field = dot(head, to_samples).reshape(points, ROWS, 2 * MC)
    power = field[:, :, :MC] ** 2 + field[:, :, MC:] ** 2
    samples = jnp.sum(weights[:, None, None] * power, axis=0)
    step = MC // BLOCKS
    twice = jnp.concatenate([samples, samples], axis=1)
    near = lax.dynamic_slice_in_dim(twice, src_index * step, MC, 1)
    interpolate = interpolation_table()
    intensity = dot(near, interpolate)
    resist = jax.nn.sigmoid(steepness * (intensity - threshold_level))
    slope = (
        2.0
        * loss_weight
        * (resist - target.astype(jnp.float32))
        * steepness
        * resist
        * (1.0 - resist)
    )
    low = dot(slope, interpolate.T)
    twice = jnp.concatenate([low, low], axis=1)
    low = lax.dynamic_slice_in_dim(twice, (src_count - src_index) * step, MC, 1)
    low = jnp.sum(everywhere(low, "src", src_count), axis=0)

    scaled = (2.0 * UNIT * weights)[:, None, None] * jnp.concatenate([low, low], axis=1)[None]
    back = dot((scaled * field).reshape(points * ROWS, 2 * MC), from_samples)
    back = back.reshape(points, ROWS, 2, KC).transpose(2, 1, 0, 3).reshape(2 * ROWS, points * KC)
    adjoint = dot(turn.T, back).reshape(2, KR, points, KC)
    adjoint = jnp.sum(adjoint * opened[None], axis=2).reshape(2 * KR, KC)

    fold_columns, fold_even, fold_odd = fold_tables()
    folded = dot(adjoint, fold_columns)
    real_even, real_odd = folded[:KR, : HALF + 1], folded[:KR, HALF + 1 :]
    imag_even, imag_odd = folded[KR:, : HALF + 1], folded[KR:, HALF + 1 :]
    even = jnp.concatenate([dot(fold_even, real_even), -dot(fold_odd, imag_even)])
    odd = jnp.concatenate([dot(fold_even, imag_odd), dot(fold_odd, real_odd)])
    kinds = 2 * (KR // 2 + 1)
    message = jnp.concatenate(
        [
            jnp.concatenate([even[:, :HALF], odd], axis=1),
            jnp.pad(even[:, HALF], (0, KC - kinds))[None],
        ]
    )
    total = jnp.sum(everywhere(message, "rows", row_count), axis=0)
    even = jnp.concatenate([total[:kinds, :HALF], total[kinds, :kinds].reshape(kinds, 1)], axis=1)
    odd = total[:kinds, HALF:]
    rows, columns, turn_cos, turn_sin = final_tables()
    rows = lax.dynamic_slice_in_dim(jnp.asarray(rows * np.float32(UNIT)), row_index * ROWS, ROWS)
    cos_part = dot(rows, even)
    sin_part = jnp.pad(dot(rows, odd), ((0, 0), (1, 0)))
    tc = lax.dynamic_slice_in_dim(jnp.asarray(turn_cos), src_index, 1)
    ts = lax.dynamic_slice_in_dim(jnp.asarray(turn_sin), src_index, 1)
    cos_turned = cos_part * tc + sin_part * ts
    sin_turned = sin_part * tc - cos_part * ts
    grad = dot(jnp.concatenate([cos_turned, sin_turned[:, 1:]], axis=1), columns)
    own_open = lax.dynamic_slice_in_dim(opening, src_index * SHARE, SHARE, 1)
    return grad * own_open * (1.0 - own_open)


def solution(mesh):
    placed = (P("rows", None), P("rows", "src"), P(), P(), P())
    return jax.shard_map(
        local, mesh=mesh, in_specs=placed, out_specs=P("rows", "src"), check_vma=False
    )
```

time: 408 us -> 98 us (0.24)
  the two profiles are of different devices: /device:TPU:6 before, /device:TPU:8 now
where the time goes in v1:
time: 98 us; the launch traced here: 97 us
  waiting for transfers between devices  41.3 us (42%)
  starting transfers between devices  30.6 us (31%)
  local copies, waits for them, and re-layouts  11.7 us (12%)
  matrix products  8.04 us (8%)
  other arithmetic  4.84 us (5%)
    all_to_all x3, waiting for transfers between devices, everywhere(): return lax.all_to_all(spread, axis, 0, 0, tiled=True)  41.3 us
    all_to_all x3, starting transfers between devices, everywhere(): return lax.all_to_all(spread, axis, 0, 0, tiled=True)  30.6 us
    dot_general x18, matrix products, dot(): jnp.dot(left, right, precision=precision, preferred_element_type=jnp.floa...  8.04 us
    unnamed x51, local copies, waits for them, and re-layouts  7.59 us
    broadcast_in_dim x3, local copies, waits for them, and re-layouts, everywhere(): spread = jnp.broadcast_to(values[None], (count,) + values.shape)  2.39 us
  transfers between devices with their start and end apart: 3, of which 3 were waited for; matrix products, arithmetic and copies ran while one was open for 4% of the time, Pallas kernels for 0%

profile of v1, /device:TPU:8, one launch (start us, length us, event | category | flops | bytes accessed | tf_op | source)
XLA Modules:
  0.0 97.0 jit_solution(15438305845102925153)
XLA Ops:
  0.0 1.2 %add_divide_fusion = f32[16,8192]{1,0:T(8,128)S(1)} fusion(f32[16,8192]{1,0:T(8,128)} %param.24), kind=kLoop, calls=%fused_computation.25 | loop fusion | flops 393216 | bytes 1048576 | tf_op jit(solution)/shard_map/div | solution.py:135
  1.4 0.8 copy-done.4
  2.2 0.6 fusion.72
  2.9 0.2 fusion.29
  3.1 0.4 copy-done.13
  3.6 0.8 broadcast_in_dim.11
  4.4 13.1 %all-to-all-start = ((f32[32,17,128]{2,1,0:T(8,128)}), f32[32,17,128]{2,1,0:T(8,128)S(1)}, u32[]{:S(2)}, u32[]{:S(2)}) async-start(f32[32,17,128]{2,1,0:T(8,128)} %broadcast_in_dim.11), calls=%async_computation | async-start | bytes 786432 | tf_op jit(solution)/shard_map/all_to_all | solution.py:115
  17.5 0.6 copy-done.17
  18.2 0.6 reduce_sum.63
  18.8 0.6 broadcast_multiply_fusion.1
  19.4 0.9 dynamic-slice_negate_fusion
  20.3 0.1 broadcast_multiply_fusion
  20.4 0.7 copy-done.15
  21.0 0.1 add.130
  21.1 0.6 copy-done.16
  21.8 0.1 multiply_multiply_fusion
  21.9 10.4 %all-to-all-done = f32[32,17,128]{2,1,0:T(8,128)S(1)} async-done(((f32[32,17,128]{2,1,0:T(8,128)}), f32[32,17,128]{2,1,0:T(8,128)S(1)}, u32[]{:S(2)}, u32[]{:S(2)}) %all-to-all-start) | async-done | bytes 278560 | tf_op jit(solution)/shard_map/all_to_all | solution.py:115
  32.3 0.2 reshape_squeeze.8
  32.5 0.9 copy-done.9
  33.4 0.4 fusion.10
  33.8 0.5 copy-done.6
  34.3 0.2 fusion.73
  34.5 0.1 add.126
  34.7 0.2 bitcast_select_fusion.1
  34.9 0.1 bitcast_select_fusion
  35.0 0.4 convolution_bitcast_fusion.1
  35.4 0.6 copy-done.3
  36.1 0.6 fusion.18
  36.7 0.1 fusion.24
  36.8 0.9 copy-done.2
  37.8 0.4 subtract_multiply_fusion
  38.2 0.3 fusion.74
  38.5 0.1 fusion.39
  38.6 0.7 broadcast_in_dim.12
  39.3 10.2 %all-to-all-start.1 = ((f32[16,16,256]{2,1,0:T(8,128)}), f32[16,16,256]{2,1,0:T(8,128)S(1)}, u32[]{:S(2)}, u32[]{:S(2)}) async-start(f32[16,16,256]{2,1,0:T(8,128)} %broadcast_in_dim.12), calls=%async_computation.1 | async-start | bytes 524288 | tf_op jit(solution)/shard_map/all_to_all | solution.py:115
  49.5 0.1 copy.52
  49.5 0.1 multiply_multiply_fusion.1
  49.6 0.1 fusion.27
  49.8 0.1 copy.58
  49.9 11.6 %all-to-all-done.1 = f32[16,16,256]{2,1,0:T(8,128)S(1)} async-done(((f32[16,16,256]{2,1,0:T(8,128)}), f32[16,16,256]{2,1,0:T(8,128)S(1)}, u32[]{:S(2)}, u32[]{:S(2)}) %all-to-all-start.1) | async-done | bytes 262176 | tf_op jit(solution)/shard_map/all_to_all | solution.py:115
  61.5 0.6 convolution_bitcast_fusion
  62.2 0.2 copy.56
  62.4 0.6 fusion
  63.0 0.3 copy-done.7
  63.3 0.2 fusion.75
  63.5 0.5 copy-done.10
  64.0 0.1 fusion.47
  64.1 0.6 copy-done.11
  64.7 0.1 fusion.8
  64.8 0.2 fusion.34
  65.0 0.2 fusion.42
  65.2 0.2 fusion.44
  65.5 0.1 pad_maximum_fusion.2
  65.6 0.9 broadcast_in_dim.14
  66.4 7.3 %all-to-all-start.2 = ((f32[32,35,128]{2,1,0:T(8,128)}), f32[32,35,128]{2,1,0:T(8,128)S(1)}, u32[]{:S(2)}, u32[]{:S(2)}) async-start(f32[32,35,128]{2,1,0:T(8,128)} %broadcast_in_dim.14), calls=%async_computation.2 | async-start | bytes 1310720 | tf_op jit(solution)/shard_map/all_to_all | solution.py:115
  73.8 0.7 fusion.64
  74.5 0.1 slice.201
  74.5 0.1 slice.203
  74.6 19.2 %all-to-all-done.2 = f32[32,35,128]{2,1,0:T(8,128)S(1)} async-done(((f32[32,35,128]{2,1,0:T(8,128)}), f32[32,35,128]{2,1,0:T(8,128)S(1)}, u32[]{:S(2)}, u32[]{:S(2)}) %all-to-all-start.2) | async-done | bytes 573472 | tf_op jit(solution)/shard_map/all_to_all | solution.py:115
  93.9 0.1 copy.60
  94.0 0.9 fusion.32
  94.9 0.9 fusion.35
  95.9 0.2 fusion.55
  96.2 0.9 fusion.2
  (57 shorter events, 0.5 us)
Async XLA Ops:
  1.2 1.0 %copy-start.4 = (f32[512,256]{1,0:T(8,128)S(1)}, f32[512,256]{1,0:T(8,128)}, u32[]{:S(2)}) copy-start(f32[512,256]{1,0:T(8,128)} %constant.87.clone) | copy-start | bytes 1572868
  2.8 0.7 copy-start.13
  2.8 0.7 copy-start.14
  4.4 27.9 %all-to-all-start = ((f32[32,17,128]{2,1,0:T(8,128)}), f32[32,17,128]{2,1,0:T(8,128)S(1)}, u32[]{:S(2)}, u32[]{:S(2)}) async-start(f32[32,17,128]{2,1,0:T(8,128)} %broadcast_in_dim.11), calls=%async_computation | async-start | bytes 786432 | tf_op jit(solution)/shard_map/all_to_all | solution.py:115
  17.5 0.7 copy-start.17
  20.4 0.7 copy-start.15
  21.1 0.7 copy-start.16
  32.5 0.9 copy-start.9
  33.4 0.9 copy-start.6
  35.0 1.0 %copy-start.3 = (f32[256,512,1]{1,0,2:T(8,128)S(1)}, f32[256,512,1]{1,0,2:T(8,128)}, u32[]{:S(2)}) copy-start(f32[256,512,1]{1,0,2:T(8,128)} %constant.120) | copy-start | bytes 1572868
  36.1 0.8 copy-start.12
  36.7 1.0 %copy-start.2 = (f32[256,512]{1,0:T(8,128)S(1)}, f32[256,512]{1,0:T(8,128)}, u32[]{:S(2)}) copy-start(f32[256,512]{1,0:T(8,128)} %constant.96.clone) | copy-start | bytes 1572868
  36.7 1.4 %copy-start.1 = (f32[512,256]{1,0:T(8,128)S(1)}, f32[512,256]{1,0:T(8,128)}, u32[]{:S(2)}) copy-start(f32[512,256]{1,0:T(8,128)} %constant.97.clone) | copy-start | bytes 1572868
  39.3 22.2 %all-to-all-start.1 = ((f32[16,16,256]{2,1,0:T(8,128)}), f32[16,16,256]{2,1,0:T(8,128)S(1)}, u32[]{:S(2)}, u32[]{:S(2)}) async-start(f32[16,16,256]{2,1,0:T(8,128)} %broadcast_in_dim.12), calls=%async_computation.1 | async-start | bytes 524288 | tf_op jit(solution)/shard_map/all_to_all | solution.py:115
  49.6 11.9 %copy-start = (f32[2,128,512,1]{2,1,0,3:T(8,128)S(1)}, f32[2,128,512,1]{2,1,0,3:T(8,128)}, u32[]{:S(2)}) copy-start(f32[2,128,512,1]{2,1,0,3:T(8,128)} %constant.121) | copy-start | bytes 1572868
  62.3 0.9 copy-start.7
  63.3 0.7 copy-start.10
  64.0 0.7 copy-start.11
  66.4 27.4 %all-to-all-start.2 = ((f32[32,35,128]{2,1,0:T(8,128)}), f32[32,35,128]{2,1,0:T(8,128)S(1)}, u32[]{:S(2)}, u32[]{:S(2)}) async-start(f32[32,35,128]{2,1,0:T(8,128)} %broadcast_in_dim.14), calls=%async_computation.2 | async-start | bytes 1310720 | tf_op jit(solution)/shard_map/all_to_all | solution.py:115
  93.9 2.0 %copy-start.5 = (f32[65,512]{1,0:T(8,128)S(1)}, f32[65,512]{1,0:T(8,128)}, u32[]{:S(2)}) copy-start(f32[65,512]{1,0:T(8,128)} %constant.118) | copy-start | bytes 399364
  94.9 1.2 %copy-start.8 = (f32[64,512]{1,0:T(8,128)S(1)}, f32[64,512]{1,0:T(8,128)}, u32[]{:S(2)}) copy-start(f32[64,512]{1,0:T(8,128)} %constant.119) | copy-start | bytes 393220

commit v2 on v1

v2 whole, which is shorter than its diff:
```python
import math

import jax
import jax.numpy as jnp
import numpy as np
from jax import lax
from jax.experimental import pallas as pl
from jax.experimental.pallas import tpu as pltpu
from jax.sharding import Mesh
from jax.sharding import PartitionSpec as P

steepness = 250.0
threshold_level = 0.25
loss_weight = 8.0
highest = lax.Precision.HIGHEST
KERNELS = True

NR = 512
NC = 8192
KR = 32
KC = 128
MC = 256
HALF = KC // 2
SHARE = 512
BLOCKS = NC // SHARE
ROWS = 16
ROW_BLOCKS = NR // ROWS
POINTS = 16
NEAR = 8
STEP = MC // BLOCKS
UNIT = 1.0 / math.sqrt(NR * NC)


def f32(table):
    return np.ascontiguousarray(np.asarray(table, dtype=np.float32))


def wave(frequency, position, period):
    angle = (np.outer(frequency, position) % period) * (2.0 * np.pi / period)
    return np.cos(angle), np.sin(angle)


def column_table():
    cos, sin = wave(np.arange(HALF + 1), np.arange(SHARE), NC)
    table = np.zeros((2 * KC, SHARE))
    table[:HALF] = cos[:HALF]
    table[HALF] = cos[HALF]
    table[HALF + 1 : KC] = -sin[1:HALF]
    table[KC] = -sin[HALF]
    return f32(table.T)


def turn_tables():
    cos, sin = wave(np.arange(BLOCKS), np.arange(HALF), BLOCKS)
    return f32(np.concatenate([cos, cos], axis=1)), f32(np.concatenate([sin, -sin], axis=1))


def spread_table():
    table = np.zeros((KC, 2 * KC))
    for frequency in range(-HALF, HALF):
        size, at = abs(frequency), frequency + HALF
        table[size, at] = 1.0
        if 0 < size < HALF:
            table[HALF + size, KC + at] = 1.0 if frequency > 0 else -1.0
    return f32(table)


def band_tables():
    cos, sin = wave(np.arange(KR) - KR // 2, np.arange(NR), NR)
    rows = np.concatenate([cos, sin]) * (UNIT * UNIT)
    split = rows.reshape(2 * KR, ROW_BLOCKS, 2, ROWS // 2)
    edge = np.concatenate([split[:, :, 0].reshape(2 * KR, -1), split[:, :, 1].reshape(2 * KR, -1)])
    return f32(rows), f32(edge)


def own_row_table():
    cos, sin = wave(np.arange(NR), np.arange(KR) - KR // 2, NR)
    cos = cos.reshape(ROW_BLOCKS, ROWS, KR)
    sin = sin.reshape(ROW_BLOCKS, ROWS, KR)
    turn = np.concatenate(
        [np.concatenate([cos, -sin], axis=2), np.concatenate([sin, cos], axis=2)], axis=1
    )
    return f32(turn)


def sample_table():
    cos, sin = wave(np.arange(KC) - HALF, np.arange(MC), MC)
    return np.block([[cos, sin], [-sin, cos]])


def interpolation_table():
    place = (np.arange(MC)[:, None] * (NC // MC) - np.arange(SHARE)[None, :]) % NC
    total = np.ones_like(place, dtype=np.float64)
    for k in range(1, HALF + 1):
        total += 2.0 * np.cos(((place * k) % NC) * (2.0 * np.pi / NC))
    return total / MC


def fold_tables():
    columns = np.zeros((KC, 2 * KC))
    for frequency in range(-HALF, HALF):
        at, size = frequency + HALF, abs(frequency)
        columns[at, size] = 1.0
        if size > 0:
            columns[at, HALF + size] = -1.0 if frequency > 0 else 1.0
    columns[0, KC] = 1.0
    columns[0, HALF] = 1.0
    rows = np.zeros((KC, 2 * KR))
    for frequency in range(-KR // 2, KR // 2):
        at, size = frequency + KR // 2, abs(frequency)
        rows[size, at] = 1.0
        if size > 0:
            rows[KR // 2 + size, KR + at] = float(np.sign(frequency))
    pick = np.zeros((8, KC))
    pick[1, 0] = 1.0
    return f32(columns), f32(rows), f32(pick)


def final_tables():
    cos, sin = wave(np.arange(NR), np.arange(KR // 2 + 1), NR)
    rows = np.zeros((NR, KC))
    rows[:, : KR // 2 + 1] = cos * UNIT
    rows[:, KR // 2 + 1 : KR + 1] = sin[:, 1:] * UNIT
    cos_y, sin_y = wave(np.arange(HALF + 1), np.arange(SHARE), NC)
    columns = np.concatenate([cos_y, sin_y[1:HALF]])
    return f32(rows.reshape(ROW_BLOCKS, ROWS, KC)), f32(columns), f32(sin_y[HALF:])


def dot(left, right):
    return jnp.dot(left, right, precision=highest, preferred_element_type=jnp.float32)


def dot_nt(left, right, precision=highest):
    return lax.dot_general(
        left, right, (((1,), (1,)), ((), ())), precision=precision, preferred_element_type=jnp.float32
    )


def split(values):
    high = values.astype(jnp.bfloat16)
    return high, (values - high.astype(jnp.float32)).astype(jnp.bfloat16)


def dot3_nt(left, right):
    high, low = split(left)
    right_high, right_low = split(right)
    one = lambda a, b: dot_nt(a, b, None)
    return one(high, right_high) + (one(high, right_low) + one(low, right_high))


def dot_tn(left, right):
    return lax.dot_general(
        left, right, (((0,), (0,)), ((), ())), precision=highest, preferred_element_type=jnp.float32
    )


def logistic(values):
    return 1.0 / (1.0 + jnp.exp(-values))


def roll(values, shift):
    if KERNELS:
        return pltpu.roll(values, shift, axis=1)
    return jnp.roll(values, shift, axis=1)


def lanes(shape):
    return lax.broadcasted_iota(jnp.int32, shape, 1)


def columns_math(mask, base, turn_cos, turn_sin):
    stacked = jnp.concatenate(
        [logistic(mask[:, SHARE * b : SHARE * (b + 1)]) for b in range(BLOCKS)], axis=0
    )
    parts = dot(stacked, base)
    main = jnp.zeros((ROWS, KC), jnp.float32)
    edge = jnp.zeros((ROWS, KC), jnp.float32)
    for b in range(BLOCKS):
        part = parts[ROWS * b : ROWS * (b + 1)]
        first = part[:, :KC]
        main = main + first * turn_cos[b : b + 1] + roll(first, HALF) * turn_sin[b : b + 1]
        edge = edge + part[:, KC:]
    return jnp.concatenate([main, edge[:8] + roll(edge[8:], 1)], axis=0)


def pupil(row_shift, col_shift):
    radius_rows = KR // 4
    radius_cols = KC // 4
    fr = lax.broadcasted_iota(jnp.int32, (KR, KC), 0) - KR // 2 + row_shift
    fc = lanes((KR, KC)) - HALF + col_shift
    limit_value = (radius_rows * radius_cols) ** 2
    inside = fr * fr * (radius_cols * radius_cols) + fc * fc * (radius_rows * radius_rows)
    return (inside <= limit_value).astype(jnp.float32)


def middle_math(
    half,
    weight,
    row_shift,
    col_shift,
    heard,
    target,
    turn,
    rows,
    rows_edge,
    spread,
    to_samples,
    interpolate,
    fold_columns,
    fold_rows,
    pick,
):
    main = jnp.concatenate([heard[b, :ROWS] for b in range(ROW_BLOCKS)], axis=0)
    edge = jnp.concatenate([heard[b, ROWS:] for b in range(ROW_BLOCKS)], axis=0)
    both = dot(dot(rows, main), spread)
    edges = dot(rows_edge, edge)
    edge_column = edges[: 2 * KR, 0:1] + edges[2 * KR :, 1:2]
    real = both[:, :KC]
    imag = both[:, KC:] - jnp.where(lanes((2 * KR, KC)) == 0, edge_column, 0.0)
    band_real = real[:KR] + imag[KR:]
    band_imag = imag[:KR] - real[KR:]

    opened = [pupil(row_shift[s], col_shift[s]) for s in range(POINTS)]
    masked = jnp.concatenate(
        [
            jnp.concatenate([band_real * opened[s], band_imag * opened[s]], axis=0)
            for s in range(POINTS)
        ],
        axis=1,
    )
    head = dot(turn, masked)
    head = jnp.concatenate(
        [
            jnp.concatenate(
                [head[:ROWS, KC * s : KC * (s + 1)], head[ROWS:, KC * s : KC * (s + 1)]], axis=1
            )
            for s in range(POINTS)
        ],
        axis=0,
    )
    field = dot(head, to_samples)
    samples = jnp.zeros((ROWS, MC), jnp.float32)
    total = 0.0
    for s in range(POINTS):
        now = field[ROWS * s : ROWS * (s + 1)]
        samples = samples + weight[s] * (now[:, :MC] * now[:, :MC] + now[:, MC:] * now[:, MC:])
        total = total + weight[s]
    share = 1.0 / jnp.full((ROWS, MC), total, jnp.float32)
    samples = samples * share
    samples = jnp.where(half == 1, roll(samples, MC // 2), samples)
    near = jnp.concatenate([samples] + [roll(samples, MC - STEP * j) for j in range(1, NEAR)], axis=0)
    intensity = dot(near, interpolate)
    resist = logistic(steepness * (intensity - threshold_level))
    slope = (
        2.0
        * loss_weight
        * (resist - target.astype(jnp.float32))
        * steepness
        * resist
        * (1.0 - resist)
    )
    lows = dot3_nt(slope, interpolate)
    low = lows[:ROWS]
    for j in range(1, NEAR):
        low = low + roll(lows[ROWS * j : ROWS * (j + 1)], STEP * j)
    low = jnp.where(half == 1, roll(low, MC // 2), low)
    low = low * share * (2.0 * UNIT)
    wide = jnp.concatenate([low, low], axis=1)
    scaled = jnp.concatenate(
        [(weight[s] * wide) * field[ROWS * s : ROWS * (s + 1)] for s in range(POINTS)], axis=0
    )
    back = dot3_nt(scaled, to_samples)
    back = jnp.concatenate(
        [
            jnp.concatenate(
                [back[ROWS * s : ROWS * (s + 1), :KC], back[ROWS * s : ROWS * (s + 1), KC:]], axis=0
            )
            for s in range(POINTS)
        ],
        axis=1,
    )
    spectra = dot_tn(turn, back)
    adjoint_real = jnp.zeros((KR, KC), jnp.float32)
    adjoint_imag = jnp.zeros((KR, KC), jnp.float32)
    for s in range(POINTS):
        now = spectra[:, KC * s : KC * (s + 1)]
        adjoint_real = adjoint_real + opened[s] * now[:KR]
        adjoint_imag = adjoint_imag + opened[s] * now[KR:]
    folded = dot(jnp.concatenate([adjoint_real, adjoint_imag], axis=0), fold_columns)
    real, imag = folded[:KR], folded[KR:]
    even = lanes((KR, 2 * KC)) <= HALF
    kinds = jnp.concatenate([jnp.where(even, real, imag), jnp.where(even, -imag, real)], axis=0)
    packed = dot(fold_rows, kinds)
    last = dot_nt(pick, packed[:, KC:])
    return jnp.concatenate([packed[:KR, :KC], packed[KR : KR + 8, :KC] + last], axis=0)


def final_math(total, mask, rows, turn_cos, turn_sin, columns, last_column):
    part = dot(rows[:, :40], total)
    edge = jnp.sum(rows * total[KR + 1 : KR + 2], axis=1, keepdims=True)
    turned = part * turn_cos + roll(part, HALF) * turn_sin
    grad = dot(turned, columns) + edge * last_column
    opening = logistic(mask)
    return grad * opening * (1.0 - opening)


VMEM = pl.BlockSpec(memory_space=pltpu.VMEM)
SMEM = pl.BlockSpec(memory_space=pltpu.SMEM)


def call(body, shape, name, scalars, arrays):
    return pl.pallas_call(
        body,
        in_specs=[SMEM] * len(scalars) + [VMEM] * len(arrays),
        out_specs=VMEM,
        out_shape=jax.ShapeDtypeStruct(shape, jnp.float32),
        name=name,
    )(*scalars, *arrays)


def pick_block(table, index):
    return lax.dynamic_index_in_dim(jnp.asarray(table), index, 0, False)


def columns_part(mask_param):
    tables = (column_table(), *turn_tables())
    if not KERNELS:
        message = columns_math(mask_param, *tables)
        return jnp.broadcast_to(message[None], (ROW_BLOCKS, *message.shape))

    def kernel(mask_ref, base_ref, cos_ref, sin_ref, out_ref):
        message = columns_math(mask_ref[...], base_ref[...], cos_ref[...], sin_ref[...])
        for b in range(ROW_BLOCKS):
            out_ref[b] = message

    return call(kernel, (ROW_BLOCKS, 24, KC), "columns_part", (), (mask_param, *tables))


def middle_part(half, row_index, weight, row_shift, col_shift, heard, target):
    target = target.reshape(NEAR * ROWS, SHARE)
    arrays = (
        heard,
        target,
        pick_block(own_row_table(), row_index),
        *band_tables(),
        spread_table(),
        f32(sample_table()),
        f32(interpolation_table()),
        *fold_tables(),
    )
    scalars = (half.reshape(1), weight, row_shift, col_shift)
    if not KERNELS:
        message = middle_math(half, *scalars[1:], *arrays)
        return jnp.broadcast_to(message[None], (8, *message.shape))

    def kernel(half_ref, weight_ref, row_ref, col_ref, heard_ref, *refs):
        *refs, out_ref = refs
        message = middle_math(
            half_ref[0], weight_ref, row_ref, col_ref, heard_ref, *[ref[...] for ref in refs]
        )
        for b in range(8):
            out_ref[b] = message

    return call(kernel, (8, 40, KC), "middle_part", scalars, arrays)


def repeat_sum(received):
    if not KERNELS:
        return jnp.broadcast_to(jnp.sum(received, axis=0)[None], received.shape)

    def kernel(in_ref, out_ref):
        total = in_ref[0]
        for b in range(1, received.shape[0]):
            total = total + in_ref[b]
        for b in range(received.shape[0]):
            out_ref[b] = total

    return call(kernel, received.shape, "repeat_sum", (), (received,))


def final_part(src_index, row_index, received, mask_param):
    rows, columns, last_column = final_tables()
    arrays = (
        received,
        lax.dynamic_slice_in_dim(mask_param, src_index * SHARE, SHARE, 1),
        pick_block(rows, row_index),
        *[pick_block(table.reshape(BLOCKS, 1, KC), src_index) for table in turn_tables()],
        columns,
        last_column,
    )
    if not KERNELS:
        return final_math(jnp.sum(received, axis=0), *arrays[1:])

    def kernel(in_ref, *refs):
        *refs, out_ref = refs
        total = in_ref[0]
        for b in range(1, received.shape[0]):
            total = total + in_ref[b]
        out_ref[...] = final_math(total, *[ref[...] for ref in refs])

    return call(kernel, (ROWS, SHARE), "final_part", (), arrays)


def swap(values, axis):
    return lax.all_to_all(values, axis, 0, 0, tiled=True)


def local(mask_param, target, source_weight, row_shift, col_shift):
    half = lax.axis_index("zh")
    src_index = lax.axis_index(("zh", "x", "c"))
    row_index = lax.axis_index(("zl", "y"))
    near = swap(jnp.broadcast_to(target[None], (NEAR, *target.shape)), ("x", "c"))
    heard = swap(columns_part(mask_param), ("zl", "y"))
    message = middle_part(half, row_index, source_weight, row_shift, col_shift, heard, near)
    message = repeat_sum(swap(message, "y"))
    return final_part(src_index, row_index, swap(message, ("zh", "zl")), mask_param)


def solution(mesh):
    fine = Mesh(mesh.devices.reshape(2, 4, 2, 4, 8), ("zh", "x", "c", "zl", "y"))
    rows, src = ("zl", "y"), ("zh", "x", "c")
    placed = (P(rows, None), P(rows, src), P(), P(), P())
    return jax.shard_map(
        local, mesh=fine, in_specs=placed, out_specs=P(rows, src), check_vma=False
    )
```

time: 98 us -> 84 us (0.86)
  the two profiles are of different devices: /device:TPU:8 before, /device:TPU:6 now
where the time goes in v2:
time: 84 us; the launch traced here: 82.6 us
  waiting for transfers between devices  30.7 us (37%)
  starting transfers between devices  29.1 us (35%)
  Pallas kernels  13.2 us (16%)
  local copies, waits for them, and re-layouts  9.48 us (11%)
    all_to_all x4, waiting for transfers between devices, swap(): return lax.all_to_all(values, axis, 0, 0, tiled=True)  30.7 us
    all_to_all x4, starting transfers between devices, swap(): return lax.all_to_all(values, axis, 0, 0, tiled=True)  29.1 us
    pallas_call x4, Pallas kernels, call(): pl.pallas_call(body, in_specs=[SMEM] * len(scalars) + [VMEM] * len(arrays...  13.2 us
    squeeze x3, local copies, waits for them, and re-layouts, pick_block(): return lax.dynamic_index_in_dim(jnp.asarray(table), index, 0, False)  3.88 us
    unnamed x8, local copies, waits for them, and re-layouts  2.76 us
  transfers between devices with their start and end apart: 4, of which 4 were waited for; matrix products, arithmetic and copies ran while one was open for 6% of the time, Pallas kernels for 3%

profile of v2, /device:TPU:6, one launch (start us, length us, event | category | flops | bytes accessed | tf_op | source)
XLA Modules:
  0.0 82.6 jit_solution(15403318324441240761)
XLA Ops:
  0.0 1.5 %broadcast_in_dim.2 = s32[8,16,512]{2,1,0:T(8,128)} broadcast(s32[16,512]{1,0:T(8,128)} %param.23), dimensions={1,2} | broadcast | bytes 294912 | tf_op jit(solution)/shard_map/broadcast_in_dim | solution.py:412
  1.5 9.2 %all-to-all-start.1 = ((s32[8,16,512]{2,1,0:T(8,128)}), s32[8,16,512]{2,1,0:T(8,128)S(1)}, u32[]{:S(2)}, u32[]{:S(2)}) async-start(s32[8,16,512]{2,1,0:T(8,128)} %broadcast_in_dim.2), calls=%async_computation.1 | async-start | bytes 524288 | tf_op jit(solution)/shard_map/all_to_all | solution.py:405
  10.6 2.8 %columns_part.1 = f32[32,24,128]{2,1,0:T(8,128)} custom-call(f32[16,8192]{1,0:T(8,128)} %mask_ref.1, f32[512,256]{1,0:T(8,128)} %constant.82.clone.base_ref, f32[16,128]{1,0:T(8,128)} %constant.83.clone.cos_ref, f32[16,128]{1,0:T(8,128)} %constant.84.clone.sin_ref), custom_call_target="tpu_custom_call" | custom-call | tf_op jit(solution)/shard_map/columns_part/pallas_call | solution.py:312
  13.4 2.6 %all-to-all-done.1 = s32[8,16,512]{2,1,0:T(8,128)S(1)} async-done(((s32[8,16,512]{2,1,0:T(8,128)}), s32[8,16,512]{2,1,0:T(8,128)S(1)}, u32[]{:S(2)}, u32[]{:S(2)}) %all-to-all-start.1) | async-done | bytes 262176 | tf_op jit(solution)/shard_map/all_to_all | solution.py:405
  16.1 0.0 copy-start.1
  16.1 0.7 copy-done.1
  16.8 8.5 %all-to-all-start = ((f32[32,24,128]{2,1,0:T(8,128)}), f32[32,24,128]{2,1,0:T(8,128)S(1)}, u32[]{:S(2)}, u32[]{:S(2)}) async-start(f32[32,24,128]{2,1,0:T(8,128)} %columns_part.1), calls=%async_computation | async-start | bytes 786432 | tf_op jit(solution)/shard_map/all_to_all | solution.py:405
  25.3 1.3 %dynamic-slice_bitcast_fusion.refs_1_ = f32[32,64]{1,0:T(8,128)} fusion(f32[32,32,64]{2,1,0:T(8,128)} %constant.85.clone, s32[]{:T(128)S(6)} %select_n.14), kind=kLoop, calls=%fused_computation | loop fusion | bytes 16388 | tf_op jit(solution)/shard_map/jit(dynamic_index_in_dim)/squeeze | solution.py:322
  26.7 13.2 %all-to-all-done.heard_ref = f32[32,24,128]{2,1,0:T(8,128)S(1)} async-done(((f32[32,24,128]{2,1,0:T(8,128)}), f32[32,24,128]{2,1,0:T(8,128)S(1)}, u32[]{:S(2)}, u32[]{:S(2)}) %all-to-all-start) | async-done | bytes 393248 | tf_op jit(solution)/shard_map/all_to_all | solution.py:405
  39.8 0.0 copy-start
  39.8 0.7 copy-done
  40.6 6.8 %middle_part.1 = f32[8,40,128]{2,1,0:T(8,128)} custom-call(s32[1]{0:T(128)} %bitcast.half_ref, f32[16]{0:T(128)} %weight_ref.1, s32[16]{0:T(128)} %row_ref.1, s32[16]{0:T(128)} %col_ref.1, f32[32,24,128]{2,1,0:T(8,128)} %copy-done, s32[128,512]{1,0:T(8,128)} %bitcast.10, f32[32,64]{1,0:T(8,128)} %dynamic-slice_bitcast_fusion.refs_1_, ...), custom_call_target="tpu_custom_call" | custom-call | tf_op jit(solution)/shard_map/middle_part/pallas_call | solution.py:312
  47.3 3.8 %all-to-all-start.2 = ((f32[8,40,128]{2,1,0:T(8,128)}), f32[8,40,128]{2,1,0:T(8,128)S(1)}, u32[]{:S(2)}, u32[]{:S(2)}) async-start(f32[8,40,128]{2,1,0:T(8,128)} %middle_part.1), calls=%async_computation.2 | async-start | bytes 327680 | tf_op jit(solution)/shard_map/all_to_all | solution.py:405
  51.1 9.4 %all-to-all-done.2.in_ref = f32[8,40,128]{2,1,0:T(8,128)S(1)} async-done(((f32[8,40,128]{2,1,0:T(8,128)}), f32[8,40,128]{2,1,0:T(8,128)S(1)}, u32[]{:S(2)}, u32[]{:S(2)}) %all-to-all-start.2) | async-done | bytes 163872 | tf_op jit(solution)/shard_map/all_to_all | solution.py:405
  60.5 0.0 copy-start.2
  60.5 0.7 copy-done.2
  61.2 1.6 %repeat_sum.1 = f32[8,40,128]{2,1,0:T(8,128)} custom-call(f32[8,40,128]{2,1,0:T(8,128)} %copy-done.2), custom_call_target="tpu_custom_call" | custom-call | tf_op jit(solution)/shard_map/repeat_sum/pallas_call | solution.py:312
  62.8 7.6 %all-to-all-start.3 = ((f32[8,40,128]{2,1,0:T(8,128)}), f32[8,40,128]{2,1,0:T(8,128)S(1)}, u32[]{:S(2)}, u32[]{:S(2)}) async-start(f32[8,40,128]{2,1,0:T(8,128)} %repeat_sum.1), calls=%async_computation.3 | async-start | bytes 327680 | tf_op jit(solution)/shard_map/all_to_all | solution.py:405
  70.4 1.3 %fusion = (f32[1,128]{1,0:T(1,128)}, f32[1,128]{1,0:T(1,128)}) fusion(f32[16,1,128]{2,1,0:T(1,128)} %constant.95.clone, s32[]{:T(128)S(6)} %select_n.16, f32[16,1,128]{2,1,0:T(1,128)} %constant.96.clone), kind=kLoop, calls=%fused_computation.5 | loop fusion | bytes 2052 | tf_op jit(solution)/shard_map/jit(dynamic_index_in_dim)/squeeze | solution.py:322
  71.6 1.3 %dynamic-slice_bitcast_fusion.1.refs_1_ = f32[16,128]{1,0:T(8,128)} fusion(f32[32,16,128]{2,1,0:T(8,128)} %constant.94.clone, s32[]{:T(128)S(6)} %select_n.14), kind=kLoop, calls=%fused_computation.1 | loop fusion | bytes 16388 | tf_op jit(solution)/shard_map/jit(dynamic_index_in_dim)/squeeze | solution.py:322
  72.9 1.4 %constant_dynamic-slice_fusion.2.refs_0_ = f32[16,512]{1,0:T(8,128)} fusion(f32[16,8192]{1,0:T(8,128)} %mask_ref.1, s32[]{:T(128)S(6)} %select_n.15), kind=kLoop, calls=%fused_computation.4 | loop fusion | bytes 65540 | tf_op jit(solution)/shard_map/dynamic_slice | solution.py:385
  74.3 5.5 %all-to-all-done.3.in_ref = f32[8,40,128]{2,1,0:T(8,128)S(1)} async-done(((f32[8,40,128]{2,1,0:T(8,128)}), f32[8,40,128]{2,1,0:T(8,128)S(1)}, u32[]{:S(2)}, u32[]{:S(2)}) %all-to-all-start.3) | async-done | bytes 163872 | tf_op jit(solution)/shard_map/all_to_all | solution.py:405
  79.8 0.0 copy-start.3
  79.8 0.7 copy-done.3
  80.5 2.1 %final_part.1 = f32[16,512]{1,0:T(8,128)} custom-call(f32[8,40,128]{2,1,0:T(8,128)} %copy-done.3, f32[16,512]{1,0:T(8,128)} %constant_dynamic-slice_fusion.2.refs_0_, f32[16,128]{1,0:T(8,128)} %dynamic-slice_bitcast_fusion.1.refs_1_, f32[1,128]{1,0:T(1,128)} %get-tuple-element.5.refs_2_, f32[1,128]{1,0:T(1,128)} %get-tuple-element.6.refs_3_, ...), custom_call_target="tpu_custom_call" | custom-call | tf_op jit(solution)/shard_map/final_part/pallas_call | solution.py:312
Async XLA Ops:
  1.5 14.6 %all-to-all-start.1 = ((s32[8,16,512]{2,1,0:T(8,128)}), s32[8,16,512]{2,1,0:T(8,128)S(1)}, u32[]{:S(2)}, u32[]{:S(2)}) async-start(s32[8,16,512]{2,1,0:T(8,128)} %broadcast_in_dim.2), calls=%async_computation.1 | async-start | bytes 524288 | tf_op jit(solution)/shard_map/all_to_all | solution.py:405
  16.1 0.7 copy-start.1
  16.8 23.1 %all-to-all-start = ((f32[32,24,128]{2,1,0:T(8,128)}), f32[32,24,128]{2,1,0:T(8,128)S(1)}, u32[]{:S(2)}, u32[]{:S(2)}) async-start(f32[32,24,128]{2,1,0:T(8,128)} %columns_part.1), calls=%async_computation | async-start | bytes 786432 | tf_op jit(solution)/shard_map/all_to_all | solution.py:405
  39.8 0.7 copy-start
  47.3 13.2 %all-to-all-start.2 = ((f32[8,40,128]{2,1,0:T(8,128)}), f32[8,40,128]{2,1,0:T(8,128)S(1)}, u32[]{:S(2)}, u32[]{:S(2)}) async-start(f32[8,40,128]{2,1,0:T(8,128)} %middle_part.1), calls=%async_computation.2 | async-start | bytes 327680 | tf_op jit(solution)/shard_map/all_to_all | solution.py:405
  60.5 0.7 copy-start.2
  62.8 17.0 %all-to-all-start.3 = ((f32[8,40,128]{2,1,0:T(8,128)}), f32[8,40,128]{2,1,0:T(8,128)S(1)}, u32[]{:S(2)}, u32[]{:S(2)}) async-start(f32[8,40,128]{2,1,0:T(8,128)} %repeat_sum.1), calls=%async_computation.3 | async-start | bytes 327680 | tf_op jit(solution)/shard_map/all_to_all | solution.py:405
  79.8 0.7 copy-start.3

commit v3 on v2

--- a/solution.py
+++ b/solution.py
@@ -309,6 +309,7 @@
 
 
 def call(body, shape, name, scalars, arrays):
+    arrays = [pltpu.with_memory_space_constraint(array, pltpu.VMEM) for array in arrays]
     return pl.pallas_call(
         body,
         in_specs=[SMEM] * len(scalars) + [VMEM] * len(arrays),

time: 84 us -> 78.8 us (0.938)
  local copies, waits for them, and re-layouts: 9.48 us -> 4.74 us
  Pallas kernels: 13.2 us -> 9.15 us
  waiting for transfers between devices: 30.7 us -> 34 us
    pallas_call x4, Pallas kernels: 13.2 us -> 9.15 us  [call(): pl.pallas_call(body, in_specs=[SMEM] * len(scalars) + [VMEM] * len(arrays...]
    all_to_all x4, waiting for transfers between devices: 30.7 us -> 34 us  [swap(): return lax.all_to_all(values, axis, 0, 0, tiled=True)]
    squeeze x3, local copies, waits for them, and re-layouts: 3.88 us -> 2.1 us  [pick_block(): return lax.dynamic_index_in_dim(jnp.asarray(table), index, 0, False)]
    unnamed x8 -> x28, local copies, waits for them, and re-layouts: 2.76 us -> 1.09 us
    dynamic_slice x1, local copies, waits for them, and re-layouts: 1.36 us -> 0.01 us  [final_part(): lax.dynamic_slice_in_dim(mask_param, src_index * SHARE, SHARE, 1)]
  transfers between devices with their start and end apart: 4 -> 4, of which waited for: 4 -> 4; matrix products, arithmetic and copies ran while one was open for 6% -> 3% of each run, Pallas kernels for 3% -> 2%
where the time goes in v3:
time: 78.8 us; the launch traced here: 77.4 us
  waiting for transfers between devices  34 us (43%)
  starting transfers between devices  29.5 us (37%)
  Pallas kernels  9.15 us (12%)
  local copies, waits for them, and re-layouts  4.74 us (6%)
    all_to_all x4, waiting for transfers between devices, swap(): return lax.all_to_all(values, axis, 0, 0, tiled=True)  34 us
    all_to_all x4, starting transfers between devices, swap(): return lax.all_to_all(values, axis, 0, 0, tiled=True)  29.5 us
    pallas_call x4, Pallas kernels, call(): pl.pallas_call(body, in_specs=[SMEM] * len(scalars) + [VMEM] * len(arrays...  9.15 us
    squeeze x3, local copies, waits for them, and re-layouts, pick_block(): return lax.dynamic_index_in_dim(jnp.asarray(table), index, 0, False)  2.1 us
  transfers between devices with their start and end apart: 4, of which 4 were waited for; matrix products, arithmetic and copies ran while one was open for 3% of the time, Pallas kernels for 2%

profile of v3, /device:TPU:6, one launch (start us, length us, event | category | flops | bytes accessed | tf_op | source)
XLA Modules:
  0.0 77.4 jit_solution(16900971943942087599)
XLA Ops:
  0.0 0.0 copy-start
  0.0 1.6 %broadcast_in_dim.2 = s32[8,16,512]{2,1,0:T(8,128)} broadcast(s32[16,512]{1,0:T(8,128)} %param.23), dimensions={1,2} | broadcast | bytes 294912 | tf_op jit(solution)/shard_map/broadcast_in_dim | solution.py:413
  1.6 0.0 copy-start.10
  1.6 0.0 copy-start.11
  1.6 9.3 %all-to-all-start.1 = ((s32[8,16,512]{2,1,0:T(8,128)}), s32[8,16,512]{2,1,0:T(8,128)S(1)}, u32[]{:S(2)}, u32[]{:S(2)}) async-start(s32[8,16,512]{2,1,0:T(8,128)} %broadcast_in_dim.2), calls=%async_computation.1 | async-start | bytes 524288 | tf_op jit(solution)/shard_map/all_to_all | solution.py:406
  10.9 0.0 copy-done
  10.9 0.0 copy-done.10
  10.9 0.0 copy-done.11
  10.9 0.0 copy-start.3
  10.9 1.0 %copy-done.3 = f32[512,256]{1,0:T(8,128)S(1)} copy-done((f32[512,256]{1,0:T(8,128)S(1)}, f32[512,256]{1,0:T(8,128)}, u32[]{:S(2)}) %copy-start.3) | copy-done | bytes 524312
  11.9 0.0 copy-start.2
  11.9 0.0 copy-start.7
  11.9 0.0 copy-start.8
  11.9 0.0 copy-start.9
  11.9 1.6 %columns_part.1 = f32[32,24,128]{2,1,0:T(8,128)} custom-call(f32[16,8192]{1,0:T(8,128)S(1)} %copy-done, f32[512,256]{1,0:T(8,128)S(1)} %copy-done.3, f32[16,128]{1,0:T(8,128)S(1)} %copy-done.10, f32[16,128]{1,0:T(8,128)S(1)} %copy-done.11), custom_call_target="tpu_custom_call" | custom-call | tf_op jit(solution)/shard_map/columns_part/pallas_call | solution.py:313
  13.5 0.0 copy-start.1
  13.5 2.7 %all-to-all-done.1 = s32[8,16,512]{2,1,0:T(8,128)S(1)} async-done(((s32[8,16,512]{2,1,0:T(8,128)}), s32[8,16,512]{2,1,0:T(8,128)S(1)}, u32[]{:S(2)}, u32[]{:S(2)}) %all-to-all-start.1) | async-done | bytes 262176 | tf_op jit(solution)/shard_map/all_to_all | solution.py:406
  16.3 0.0 copy-start.5
  16.3 0.0 copy-start.6
  16.3 8.7 %all-to-all-start = ((f32[32,24,128]{2,1,0:T(8,128)}), f32[32,24,128]{2,1,0:T(8,128)S(1)}, u32[]{:S(2)}, u32[]{:S(2)}) async-start(f32[32,24,128]{2,1,0:T(8,128)} %columns_part.1), calls=%async_computation | async-start | bytes 786432 | tf_op jit(solution)/shard_map/all_to_all | solution.py:406
  25.0 0.0 copy-start.12
  25.0 0.7 dynamic-slice_bitcast_fusion.refs_1_
  25.7 13.8 %all-to-all-done.heard_ref = f32[32,24,128]{2,1,0:T(8,128)S(1)} async-done(((f32[32,24,128]{2,1,0:T(8,128)}), f32[32,24,128]{2,1,0:T(8,128)S(1)}, u32[]{:S(2)}, u32[]{:S(2)}) %all-to-all-start) | async-done | bytes 393248 | tf_op jit(solution)/shard_map/all_to_all | solution.py:406
  39.5 0.0 copy-done.2
  39.5 0.0 copy-done.7
  39.5 0.0 copy-done.8
  39.5 0.0 copy-done.9
  39.5 0.0 copy-done.1
  39.5 0.0 copy-done.5
  39.5 0.0 copy-done.6
  39.5 0.0 copy-done.12
  39.5 5.8 %middle_part.1 = f32[8,40,128]{2,1,0:T(8,128)} custom-call(s32[1]{0:T(128)} %bitcast.half_ref, f32[16]{0:T(128)} %weight_ref.1, s32[16]{0:T(128)} %row_ref.1, s32[16]{0:T(128)} %col_ref.1, f32[32,24,128]{2,1,0:T(8,128)S(1)} %all-to-all-done.heard_ref, s32[128,512]{1,0:T(8,128)S(1)} %bitcast.10, f32[32,64]{1,0:T(8,128)S(1)} %dynamic-slice_bitcast_fusion.refs_1_, ...), custom_call_target="tpu_custom_call" | custom-call | tf_op jit(solution)/shard_map/middle_part/pallas_call | solution.py:313
  45.3 3.8 %all-to-all-start.2 = ((f32[8,40,128]{2,1,0:T(8,128)}), f32[8,40,128]{2,1,0:T(8,128)S(1)}, u32[]{:S(2)}, u32[]{:S(2)}) async-start(f32[8,40,128]{2,1,0:T(8,128)} %middle_part.1), calls=%async_computation.2 | async-start | bytes 327680 | tf_op jit(solution)/shard_map/all_to_all | solution.py:406
  49.1 9.4 %all-to-all-done.2.in_ref = f32[8,40,128]{2,1,0:T(8,128)S(1)} async-done(((f32[8,40,128]{2,1,0:T(8,128)}), f32[8,40,128]{2,1,0:T(8,128)S(1)}, u32[]{:S(2)}, u32[]{:S(2)}) %all-to-all-start.2) | async-done | bytes 163872 | tf_op jit(solution)/shard_map/all_to_all | solution.py:406
  58.5 0.7 repeat_sum.1
  59.2 0.0 copy-start.4
  59.2 7.7 %all-to-all-start.3 = ((f32[8,40,128]{2,1,0:T(8,128)}), f32[8,40,128]{2,1,0:T(8,128)S(1)}, u32[]{:S(2)}, u32[]{:S(2)}) async-start(f32[8,40,128]{2,1,0:T(8,128)} %repeat_sum.1), calls=%async_computation.3 | async-start | bytes 327680 | tf_op jit(solution)/shard_map/all_to_all | solution.py:406
  66.9 0.7 fusion
  67.6 0.7 dynamic-slice_bitcast_fusion.1.refs_1_
  68.3 0.0 copy-start.13
  68.3 8.1 %all-to-all-done.3.in_ref = f32[8,40,128]{2,1,0:T(8,128)S(1)} async-done(((f32[8,40,128]{2,1,0:T(8,128)}), f32[8,40,128]{2,1,0:T(8,128)S(1)}, u32[]{:S(2)}, u32[]{:S(2)}) %all-to-all-start.3) | async-done | bytes 163872 | tf_op jit(solution)/shard_map/all_to_all | solution.py:406
  76.4 0.0 copy-done.4
  76.4 0.0 copy-done.13
  76.4 1.1 %final_part.1 = f32[16,512]{1,0:T(8,128)} custom-call(f32[8,40,128]{2,1,0:T(8,128)S(1)} %all-to-all-done.3.in_ref, f32[16,512]{1,0:T(8,128)S(1)} %constant_dynamic-slice_fusion.2.refs_0_, f32[16,128]{1,0:T(8,128)S(1)} %dynamic-slice_bitcast_fusion.1.refs_1_, f32[1,128]{1,0:T(1,128)S(1)} %get-tuple-element.5.refs_2_, f32[1,128]{1,0:T(1,128)S(1)} %get-tuple-element.6.refs_3_, ...), custom_call_target="tpu_custom_call" | custom-call | tf_op jit(solution)/shard_map/final_part/pallas_call | solution.py:313
  (1 shorter events, 0.0 us)
Async XLA Ops:
  0.0 10.9 %copy-start = (f32[16,8192]{1,0:T(8,128)S(1)}, f32[16,8192]{1,0:T(8,128)}, u32[]{:S(2)}) copy-start(f32[16,8192]{1,0:T(8,128)} %mask_ref.1) | copy-start | bytes 1572868
  1.6 9.3 %copy-start.10 = (f32[16,128]{1,0:T(8,128)S(1)}, f32[16,128]{1,0:T(8,128)}, u32[]{:S(2)}) copy-start(f32[16,128]{1,0:T(8,128)} %constant.83.clone.cos_ref) | copy-start | bytes 24580
  1.6 9.3 %copy-start.11 = (f32[16,128]{1,0:T(8,128)S(1)}, f32[16,128]{1,0:T(8,128)}, u32[]{:S(2)}) copy-start(f32[16,128]{1,0:T(8,128)} %constant.84.clone.sin_ref) | copy-start | bytes 24580
  1.6 14.7 %all-to-all-start.1 = ((s32[8,16,512]{2,1,0:T(8,128)}), s32[8,16,512]{2,1,0:T(8,128)S(1)}, u32[]{:S(2)}, u32[]{:S(2)}) async-start(s32[8,16,512]{2,1,0:T(8,128)} %broadcast_in_dim.2), calls=%async_computation.1 | async-start | bytes 524288 | tf_op jit(solution)/shard_map/all_to_all | solution.py:406
  10.9 1.0 %copy-start.3 = (f32[512,256]{1,0:T(8,128)S(1)}, f32[512,256]{1,0:T(8,128)}, u32[]{:S(2)}) copy-start(f32[512,256]{1,0:T(8,128)} %constant.82.clone.base_ref) | copy-start | bytes 1572868
  11.9 27.6 %copy-start.2 = (f32[256,512]{1,0:T(8,128)S(1)}, f32[256,512]{1,0:T(8,128)}, u32[]{:S(2)}) copy-start(f32[256,512]{1,0:T(8,128)} %constant.90.clone.refs_6_) | copy-start | bytes 1572868
  11.9 27.6 %copy-start.7 = (f32[128,256]{1,0:T(8,128)S(1)}, f32[128,256]{1,0:T(8,128)}, u32[]{:S(2)}) copy-start(f32[128,256]{1,0:T(8,128)} %constant.88.clone.refs_4_) | copy-start | bytes 393220
  11.9 27.6 %copy-start.8 = (f32[128,256]{1,0:T(8,128)S(1)}, f32[128,256]{1,0:T(8,128)}, u32[]{:S(2)}) copy-start(f32[128,256]{1,0:T(8,128)} %constant.91.clone.refs_7_) | copy-start | bytes 393220
  11.9 27.6 %copy-start.9 = (f32[128,64]{1,0:T(8,128)S(1)}, f32[128,64]{1,0:T(8,128)}, u32[]{:S(2)}) copy-start(f32[128,64]{1,0:T(8,128)} %constant.92.clone.refs_8_) | copy-start | bytes 98308
  13.5 26.0 %copy-start.1 = (f32[256,512]{1,0:T(8,128)S(1)}, f32[256,512]{1,0:T(8,128)}, u32[]{:S(2)}) copy-start(f32[256,512]{1,0:T(8,128)} %constant.89.clone.refs_5_) | copy-start | bytes 1572868
  16.3 23.2 %copy-start.5 = (f32[64,512]{1,0:T(8,128)S(1)}, f32[64,512]{1,0:T(8,128)}, u32[]{:S(2)}) copy-start(f32[64,512]{1,0:T(8,128)} %constant.86.clone.refs_2_) | copy-start | bytes 393220
  16.3 23.2 %copy-start.6 = (f32[128,256]{1,0:T(8,128)S(1)}, f32[128,256]{1,0:T(8,128)}, u32[]{:S(2)}) copy-start(f32[128,256]{1,0:T(8,128)} %constant.87.clone.refs_3_) | copy-start | bytes 393220
  16.3 23.2 %all-to-all-start = ((f32[32,24,128]{2,1,0:T(8,128)}), f32[32,24,128]{2,1,0:T(8,128)S(1)}, u32[]{:S(2)}, u32[]{:S(2)}) async-start(f32[32,24,128]{2,1,0:T(8,128)} %columns_part.1), calls=%async_computation | async-start | bytes 786432 | tf_op jit(solution)/shard_map/all_to_all | solution.py:406
  25.0 14.6 %copy-start.12 = (f32[8,128]{1,0:T(8,128)S(1)}, f32[8,128]{1,0:T(8,128)}, u32[]{:S(2)}) copy-start(f32[8,128]{1,0:T(8,128)} %constant.93.clone.refs_9_) | copy-start | bytes 12292
  45.3 13.2 %all-to-all-start.2 = ((f32[8,40,128]{2,1,0:T(8,128)}), f32[8,40,128]{2,1,0:T(8,128)S(1)}, u32[]{:S(2)}, u32[]{:S(2)}) async-start(f32[8,40,128]{2,1,0:T(8,128)} %middle_part.1), calls=%async_computation.2 | async-start | bytes 327680 | tf_op jit(solution)/shard_map/all_to_all | solution.py:406
  59.2 17.2 %copy-start.4 = (f32[128,512]{1,0:T(8,128)S(1)}, f32[128,512]{1,0:T(8,128)}, u32[]{:S(2)}) copy-start(f32[128,512]{1,0:T(8,128)} %constant.97.clone.refs_4_) | copy-start | bytes 786436
  59.2 17.1 %all-to-all-start.3 = ((f32[8,40,128]{2,1,0:T(8,128)}), f32[8,40,128]{2,1,0:T(8,128)S(1)}, u32[]{:S(2)}, u32[]{:S(2)}) async-start(f32[8,40,128]{2,1,0:T(8,128)} %repeat_sum.1), calls=%async_computation.3 | async-start | bytes 327680 | tf_op jit(solution)/shard_map/all_to_all | solution.py:406
  68.3 8.1 %copy-start.13 = (f32[1,512]{1,0:T(1,128)S(1)}, f32[1,512]{1,0:T(1,128)}, u32[]{:S(2)}) copy-start(f32[1,512]{1,0:T(1,128)} %constant.98.clone.refs_5_) | copy-start | bytes 6148

commit v4 on v3

--- a/solution.py
+++ b/solution.py
@@ -28,6 +28,7 @@
 POINTS = 16
 NEAR = 8
 STEP = MC // BLOCKS
+LINES = ROWS + 1
 UNIT = 1.0 / math.sqrt(NR * NC)
 
 
@@ -47,7 +48,7 @@
     table[HALF] = cos[HALF]
     table[HALF + 1 : KC] = -sin[1:HALF]
     table[KC] = -sin[HALF]
-    return f32(table.T)
+    return f32(table[: KC + 8])
 
 
 def turn_tables():
@@ -66,11 +67,12 @@
 
 
 def band_tables():
-    cos, sin = wave(np.arange(KR) - KR // 2, np.arange(NR), NR)
-    rows = np.concatenate([cos, sin]) * (UNIT * UNIT)
-    split = rows.reshape(2 * KR, ROW_BLOCKS, 2, ROWS // 2)
-    edge = np.concatenate([split[:, :, 0].reshape(2 * KR, -1), split[:, :, 1].reshape(2 * KR, -1)])
-    return f32(rows), f32(edge)
+    frequency = np.arange(KR) - KR // 2
+    rows = np.concatenate(wave(frequency, np.arange(NR), NR)) * (UNIT * UNIT)
+    inner = np.zeros((2 * KR, KC))
+    inner[:, :ROWS] = np.concatenate(wave(frequency, np.arange(ROWS), NR)) * (UNIT * UNIT)
+    outer = np.concatenate(wave(frequency, np.arange(ROW_BLOCKS) * ROWS, NR))
+    return f32(rows), f32(inner), f32(outer)
 
 
 def own_row_table():
@@ -168,19 +170,20 @@
     return lax.broadcasted_iota(jnp.int32, shape, 1)
 
 
-def columns_math(mask, base, turn_cos, turn_sin):
+def columns_math(mask, base, turn_cos, turn_sin, pick):
     stacked = jnp.concatenate(
         [logistic(mask[:, SHARE * b : SHARE * (b + 1)]) for b in range(BLOCKS)], axis=0
     )
-    parts = dot(stacked, base)
+    parts = dot_nt(stacked, base)
     main = jnp.zeros((ROWS, KC), jnp.float32)
-    edge = jnp.zeros((ROWS, KC), jnp.float32)
+    edge = jnp.zeros((ROWS, 8), jnp.float32)
     for b in range(BLOCKS):
         part = parts[ROWS * b : ROWS * (b + 1)]
         first = part[:, :KC]
         main = main + first * turn_cos[b : b + 1] + roll(first, HALF) * turn_sin[b : b + 1]
         edge = edge + part[:, KC:]
-    return jnp.concatenate([main, edge[:8] + roll(edge[8:], 1)], axis=0)
+    edge = jnp.concatenate([edge, jnp.zeros((KC - ROWS, 8), jnp.float32)], axis=0)
+    return main, dot_nt(pick[:, :8], edge)[1:2]
 
 
 def pupil(row_shift, col_shift):
@@ -198,11 +201,13 @@
     weight,
     row_shift,
     col_shift,
-    heard,
+    main,
+    edge,
     target,
     turn,
     rows,
-    rows_edge,
+    inner,
+    outer,
     spread,
     to_samples,
     interpolate,
@@ -210,11 +215,13 @@
     fold_rows,
     pick,
 ):
-    main = jnp.concatenate([heard[b, :ROWS] for b in range(ROW_BLOCKS)], axis=0)
-    edge = jnp.concatenate([heard[b, ROWS:] for b in range(ROW_BLOCKS)], axis=0)
     both = dot(dot(rows, main), spread)
-    edges = dot(rows_edge, edge)
-    edge_column = edges[: 2 * KR, 0:1] + edges[2 * KR :, 1:2]
+    inside = dot_nt(inner, edge)
+    in_cos, in_sin = inside[:KR], inside[KR:]
+    out_cos, out_sin = outer[:KR], outer[KR:]
+    edge_cos = jnp.sum(out_cos * in_cos - out_sin * in_sin, axis=1, keepdims=True)
+    edge_sin = jnp.sum(out_sin * in_cos + out_cos * in_sin, axis=1, keepdims=True)
+    edge_column = jnp.concatenate([edge_cos, edge_sin], axis=0)
     real = both[:, :KC]
     imag = both[:, KC:] - jnp.where(lanes((2 * KR, KC)) == 0, edge_column, 0.0)
     band_real = real[:KR] + imag[KR:]
@@ -308,41 +315,51 @@
 SMEM = pl.BlockSpec(memory_space=pltpu.SMEM)
 
 
-def call(body, shape, name, scalars, arrays):
+def call(body, outputs, name, scalars, arrays):
     arrays = [pltpu.with_memory_space_constraint(array, pltpu.VMEM) for array in arrays]
     return pl.pallas_call(
         body,
         in_specs=[SMEM] * len(scalars) + [VMEM] * len(arrays),
-        out_specs=VMEM,
-        out_shape=jax.ShapeDtypeStruct(shape, jnp.float32),
+        out_specs=jax.tree.map(lambda _: VMEM, outputs),
+        out_shape=outputs,
         name=name,
     )(*scalars, *arrays)
 
 
+def plain(*shape):
+    return jax.ShapeDtypeStruct(shape, jnp.float32)
+
+
 def pick_block(table, index):
     return lax.dynamic_index_in_dim(jnp.asarray(table), index, 0, False)
 
 
 def columns_part(mask_param):
-    tables = (column_table(), *turn_tables())
+    tables = (column_table(), *turn_tables(), fold_tables()[2])
     if not KERNELS:
-        message = columns_math(mask_param, *tables)
-        return jnp.broadcast_to(message[None], (ROW_BLOCKS, *message.shape))
-
-    def kernel(mask_ref, base_ref, cos_ref, sin_ref, out_ref):
-        message = columns_math(mask_ref[...], base_ref[...], cos_ref[...], sin_ref[...])
+        return repeated(jnp.concatenate(columns_math(mask_param, *tables)), ROW_BLOCKS)
+
+    def kernel(mask_ref, *refs):
+        *refs, out_ref = refs
+        main, edge = columns_math(mask_ref[...], *[ref[...] for ref in refs])
         for b in range(ROW_BLOCKS):
-            out_ref[b] = message
-
-    return call(kernel, (ROW_BLOCKS, 24, KC), "columns_part", (), (mask_param, *tables))
-
-
-def middle_part(half, row_index, weight, row_shift, col_shift, heard, target):
-    target = target.reshape(NEAR * ROWS, SHARE)
+            out_ref[LINES * b : LINES * b + ROWS] = main
+            out_ref[LINES * b + ROWS : LINES * (b + 1)] = edge
+
+    sent = call(kernel, plain(ROW_BLOCKS * LINES, KC), "columns_part", (), (mask_param, *tables))
+    return sent.reshape(ROW_BLOCKS, 1, LINES * KC)
+
+
+def repeated(values, count):
+    return jnp.broadcast_to(values[None], (count, *values.shape))
+
+
+def middle_part(half, weight, row_shift, col_shift, heard, target, turn):
+    heard = heard.reshape(ROW_BLOCKS * LINES, KC)
     arrays = (
         heard,
-        target,
-        pick_block(own_row_table(), row_index),
+        target.reshape(NEAR * ROWS, SHARE),
+        turn,
         *band_tables(),
         spread_table(),
         f32(sample_table()),
@@ -351,18 +368,23 @@
     )
     scalars = (half.reshape(1), weight, row_shift, col_shift)
     if not KERNELS:
-        message = middle_math(half, *scalars[1:], *arrays)
-        return jnp.broadcast_to(message[None], (8, *message.shape))
+        lines = heard.reshape(ROW_BLOCKS, LINES, KC)
+        main, edge = lines[:, :ROWS].reshape(NR, KC), lines[:, ROWS]
+        return repeated(middle_math(half, *scalars[1:], main, edge, *arrays[1:]), 8)
 
     def kernel(half_ref, weight_ref, row_ref, col_ref, heard_ref, *refs):
         *refs, out_ref = refs
+        main = jnp.concatenate(
+            [heard_ref[LINES * b : LINES * b + ROWS] for b in range(ROW_BLOCKS)], axis=0
+        )
+        edge = heard_ref[pl.ds(ROWS, ROW_BLOCKS, stride=LINES)]
         message = middle_math(
-            half_ref[0], weight_ref, row_ref, col_ref, heard_ref, *[ref[...] for ref in refs]
+            half_ref[0], weight_ref, row_ref, col_ref, main, edge, *[ref[...] for ref in refs]
         )
         for b in range(8):
             out_ref[b] = message
 
-    return call(kernel, (8, 40, KC), "middle_part", scalars, arrays)
+    return call(kernel, plain(8, 40, KC), "middle_part", scalars, arrays)
 
 
 def repeat_sum(received):
@@ -376,7 +398,7 @@
         for b in range(received.shape[0]):
             out_ref[b] = total
 
-    return call(kernel, received.shape, "repeat_sum", (), (received,))
+    return call(kernel, plain(*received.shape), "repeat_sum", (), (received,))
 
 
 def final_part(src_index, row_index, received, mask_param):
@@ -399,7 +421,7 @@
             total = total + in_ref[b]
         out_ref[...] = final_math(total, *[ref[...] for ref in refs])
 
-    return call(kernel, (ROWS, SHARE), "final_part", (), arrays)
+    return call(kernel, plain(ROWS, SHARE), "final_part", (), arrays)
 
 
 def swap(values, axis):
@@ -410,10 +432,11 @@
     half = lax.axis_index("zh")
     src_index = lax.axis_index(("zh", "x", "c"))
     row_index = lax.axis_index(("zl", "y"))
-    near = swap(jnp.broadcast_to(target[None], (NEAR, *target.shape)), ("x", "c"))
+    source = (source_weight, row_shift, col_shift)
+    turn = pick_block(own_row_table(), row_index)
+    near = swap(repeated(target, NEAR), ("x", "c"))
     heard = swap(columns_part(mask_param), ("zl", "y"))
-    message = middle_part(half, row_index, source_weight, row_shift, col_shift, heard, near)
-    message = repeat_sum(swap(message, "y"))
+    message = repeat_sum(swap(middle_part(half, *source, heard, near, turn), "y"))
     return final_part(src_index, row_index, swap(message, ("zh", "zl")), mask_param)
 
 

time: 78.8 us -> 76.2 us (0.967)
  waiting for transfers between devices: 34 us -> 32.8 us
  local copies, waits for them, and re-layouts: 4.74 us -> 3.75 us
    all_to_all x4, waiting for transfers between devices: 34 us -> 32.8 us  [swap(): return lax.all_to_all(values, axis, 0, 0, tiled=True)]
    unnamed x28 -> x30, local copies, waits for them, and re-layouts: 1.09 us -> 0.07 us
where the time goes in v4:
time: 76.2 us; the launch traced here: 74.8 us
  waiting for transfers between devices  32.8 us (43%)
  starting transfers between devices  29.2 us (38%)
  Pallas kernels  8.94 us (12%)
  local copies, waits for them, and re-layouts  3.75 us (5%)
    all_to_all x4, waiting for transfers between devices, swap(): return lax.all_to_all(values, axis, 0, 0, tiled=True)  32.8 us
    all_to_all x4, starting transfers between devices, swap(): return lax.all_to_all(values, axis, 0, 0, tiled=True)  29.2 us
    pallas_call x4, Pallas kernels, call(): pl.pallas_call(body, in_specs=[SMEM] * len(scalars) + [VMEM] * len(arrays...  8.94 us
    squeeze x3, local copies, waits for them, and re-layouts, pick_block(): return lax.dynamic_index_in_dim(jnp.asarray(table), index, 0, False)  2.13 us
    broadcast_in_dim x1, local copies, waits for them, and re-layouts, repeated(): return jnp.broadcast_to(values[None], (count, *values.shape))  1.55 us
  transfers between devices with their start and end apart: 4, of which 4 were waited for; matrix products, arithmetic and copies ran while one was open for 3% of the time, Pallas kernels for 2%

profile of v4, /device:TPU:6, one launch (start us, length us, event | category | flops | bytes accessed | tf_op | source)
XLA Modules:
  0.0 74.8 jit_solution(2172578325266624562)
XLA Ops:
  0.0 0.0 copy-start.13
  0.0 0.0 copy-start
  0.0 1.5 %broadcast_in_dim.2 = s32[8,16,512]{2,1,0:T(8,128)} broadcast(s32[16,512]{1,0:T(8,128)} %param.25), dimensions={1,2} | broadcast | bytes 294912 | tf_op jit(solution)/shard_map/broadcast_in_dim | solution.py:354
  1.6 0.0 copy-start.3
  1.6 0.0 copy-start.11
  1.6 0.0 copy-start.12
  1.6 9.3 %all-to-all-start.1 = ((s32[8,16,512]{2,1,0:T(8,128)}), s32[8,16,512]{2,1,0:T(8,128)S(1)}, u32[]{:S(2)}, u32[]{:S(2)}) async-start(s32[8,16,512]{2,1,0:T(8,128)} %broadcast_in_dim.2), calls=%async_computation.1 | async-start | bytes 524288 | tf_op jit(solution)/shard_map/all_to_all | solution.py:428
  10.9 0.0 copy-done.13
  10.9 0.0 copy-done
  10.9 0.0 copy-done.3
  10.9 0.0 copy-done.11
  10.9 0.0 copy-done.12
  10.9 0.0 copy-start.2
  10.9 0.0 copy-start.5
  10.9 0.0 copy-start.6
  10.9 0.0 copy-start.7
  11.0 0.0 copy-start.10
  11.0 1.5 %columns_part.1 = f32[544,128]{1,0:T(8,128)} custom-call(f32[16,8192]{1,0:T(8,128)S(1)} %copy-done, f32[136,512]{1,0:T(8,128)S(1)} %copy-done.3, f32[16,128]{1,0:T(8,128)S(1)} %copy-done.12, f32[16,128]{1,0:T(8,128)S(1)} %copy-done.13, f32[8,128]{1,0:T(8,128)S(1)} %copy-done.11), custom_call_target="tpu_custom_call" | custom-call | tf_op jit(solution)/shard_map/columns_part/pallas_call | solution.py:320
  12.5 0.0 copy-start.1
  12.5 3.8 %all-to-all-done.1 = s32[8,16,512]{2,1,0:T(8,128)S(1)} async-done(((s32[8,16,512]{2,1,0:T(8,128)}), s32[8,16,512]{2,1,0:T(8,128)S(1)}, u32[]{:S(2)}, u32[]{:S(2)}) %all-to-all-start.1) | async-done | bytes 262176 | tf_op jit(solution)/shard_map/all_to_all | solution.py:428
  16.3 0.0 copy-start.9
  16.3 8.7 %all-to-all-start = ((f32[32,1,2176]{2,1,0:T(1,128)}), f32[32,1,2176]{2,1,0:T(1,128)S(1)}, u32[]{:S(2)}, u32[]{:S(2)}) async-start(f32[32,1,2176]{2,1,0:T(1,128)} %bitcast.14), calls=%async_computation | async-start | bytes 557056 | tf_op jit(solution)/shard_map/all_to_all | solution.py:428
  25.0 0.0 copy-start.8
  25.0 0.8 %dynamic-slice_bitcast_fusion.refs_1_ = f32[32,64]{1,0:T(8,128)S(1)} fusion(f32[32,32,64]{2,1,0:T(8,128)} %constant.84.clone, s32[]{:T(128)S(6)} %select_n.14), kind=kLoop, calls=%fused_computation | loop fusion | bytes 16388 | tf_op jit(solution)/shard_map/jit(dynamic_index_in_dim)/squeeze | solution.py:334
  25.7 11.6 %all-to-all-done = f32[32,1,2176]{2,1,0:T(1,128)S(1)} async-done(((f32[32,1,2176]{2,1,0:T(1,128)}), f32[32,1,2176]{2,1,0:T(1,128)S(1)}, u32[]{:S(2)}, u32[]{:S(2)}) %all-to-all-start) | async-done | bytes 278560 | tf_op jit(solution)/shard_map/all_to_all | solution.py:428
  37.3 0.0 copy-done.2
  37.3 0.0 copy-done.5
  37.3 0.0 copy-done.6
  37.3 0.0 copy-done.7
  37.3 0.0 copy-done.10
  37.3 0.0 copy-done.1
  37.3 0.0 copy-done.9
  37.3 0.0 copy-done.8
  37.4 5.7 %middle_part.1 = f32[8,40,128]{2,1,0:T(8,128)} custom-call(s32[1]{0:T(128)} %bitcast.half_ref, f32[16]{0:T(128)} %weight_ref.1, s32[16]{0:T(128)} %row_ref.1, s32[16]{0:T(128)} %col_ref.1, f32[544,128]{1,0:T(8,128)S(1)} %bitcast.12, s32[128,512]{1,0:T(8,128)S(1)} %bitcast.13, f32[32,64]{1,0:T(8,128)S(1)} %dynamic-slice_bitcast_fusion.refs_1_, ...), custom_call_target="tpu_custom_call" | custom-call | tf_op jit(solution)/shard_map/middle_part/pallas_call | solution.py:320
  43.0 3.5 %all-to-all-start.2 = ((f32[8,40,128]{2,1,0:T(8,128)}), f32[8,40,128]{2,1,0:T(8,128)S(1)}, u32[]{:S(2)}, u32[]{:S(2)}) async-start(f32[8,40,128]{2,1,0:T(8,128)} %middle_part.1), calls=%async_computation.2 | async-start | bytes 327680 | tf_op jit(solution)/shard_map/all_to_all | solution.py:428
  46.5 9.4 %all-to-all-done.2.in_ref = f32[8,40,128]{2,1,0:T(8,128)S(1)} async-done(((f32[8,40,128]{2,1,0:T(8,128)}), f32[8,40,128]{2,1,0:T(8,128)S(1)}, u32[]{:S(2)}, u32[]{:S(2)}) %all-to-all-start.2) | async-done | bytes 163872 | tf_op jit(solution)/shard_map/all_to_all | solution.py:428
  55.9 0.7 repeat_sum.1
  56.6 0.0 copy-start.4
  56.6 7.7 %all-to-all-start.3 = ((f32[8,40,128]{2,1,0:T(8,128)}), f32[8,40,128]{2,1,0:T(8,128)S(1)}, u32[]{:S(2)}, u32[]{:S(2)}) async-start(f32[8,40,128]{2,1,0:T(8,128)} %repeat_sum.1), calls=%async_computation.3 | async-start | bytes 327680 | tf_op jit(solution)/shard_map/all_to_all | solution.py:428
  64.3 0.7 fusion
  65.0 0.7 dynamic-slice_bitcast_fusion.1.refs_1_
  65.7 0.0 copy-start.14
  65.7 8.1 %all-to-all-done.3.in_ref = f32[8,40,128]{2,1,0:T(8,128)S(1)} async-done(((f32[8,40,128]{2,1,0:T(8,128)}), f32[8,40,128]{2,1,0:T(8,128)S(1)}, u32[]{:S(2)}, u32[]{:S(2)}) %all-to-all-start.3) | async-done | bytes 163872 | tf_op jit(solution)/shard_map/all_to_all | solution.py:428
  73.8 0.0 copy-done.4
  73.8 0.0 copy-done.14
  73.8 1.1 %final_part.1 = f32[16,512]{1,0:T(8,128)} custom-call(f32[8,40,128]{2,1,0:T(8,128)S(1)} %all-to-all-done.3.in_ref, f32[16,512]{1,0:T(8,128)S(1)} %constant_dynamic-slice_fusion.2.refs_0_, f32[16,128]{1,0:T(8,128)S(1)} %dynamic-slice_bitcast_fusion.1.refs_1_, f32[1,128]{1,0:T(1,128)S(1)} %get-tuple-element.5.refs_2_, f32[1,128]{1,0:T(1,128)S(1)} %get-tuple-element.6.refs_3_, ...), custom_call_target="tpu_custom_call" | custom-call | tf_op jit(solution)/shard_map/final_part/pallas_call | solution.py:320
  (1 shorter events, 0.0 us)
Async XLA Ops:
  0.0 10.9 %copy-start.13 = (f32[16,128]{1,0:T(8,128)S(1)}, f32[16,128]{1,0:T(8,128)}, u32[]{:S(2)}) copy-start(f32[16,128]{1,0:T(8,128)} %constant.87.clone.refs_2_) | copy-start | bytes 24580
  0.0 10.9 %copy-start = (f32[16,8192]{1,0:T(8,128)S(1)}, f32[16,8192]{1,0:T(8,128)}, u32[]{:S(2)}) copy-start(f32[16,8192]{1,0:T(8,128)} %mask_ref.1) | copy-start | bytes 1572868
  1.6 9.3 %copy-start.3 = (f32[136,512]{1,0:T(8,128)S(1)}, f32[136,512]{1,0:T(8,128)}, u32[]{:S(2)}) copy-start(f32[136,512]{1,0:T(8,128)} %constant.85.clone.refs_0_) | copy-start | bytes 835588
  1.6 9.3 %copy-start.11 = (f32[8,128]{1,0:T(8,128)S(1)}, f32[8,128]{1,0:T(8,128)}, u32[]{:S(2)}) copy-start(f32[8,128]{1,0:T(8,128)} %constant.88.clone.refs_3_.refs_10_) | copy-start | bytes 12292
  1.6 9.3 %copy-start.12 = (f32[16,128]{1,0:T(8,128)S(1)}, f32[16,128]{1,0:T(8,128)}, u32[]{:S(2)}) copy-start(f32[16,128]{1,0:T(8,128)} %constant.86.clone.refs_1_) | copy-start | bytes 24580
  1.6 14.7 %all-to-all-start.1 = ((s32[8,16,512]{2,1,0:T(8,128)}), s32[8,16,512]{2,1,0:T(8,128)S(1)}, u32[]{:S(2)}, u32[]{:S(2)}) async-start(s32[8,16,512]{2,1,0:T(8,128)} %broadcast_in_dim.2), calls=%async_computation.1 | async-start | bytes 524288 | tf_op jit(solution)/shard_map/all_to_all | solution.py:428
  10.9 26.4 %copy-start.2 = (f32[256,512]{1,0:T(8,128)S(1)}, f32[256,512]{1,0:T(8,128)}, u32[]{:S(2)}) copy-start(f32[256,512]{1,0:T(8,128)} %constant.94.clone.refs_7_) | copy-start | bytes 1572868
  10.9 26.4 %copy-start.5 = (f32[64,512]{1,0:T(8,128)S(1)}, f32[64,512]{1,0:T(8,128)}, u32[]{:S(2)}) copy-start(f32[64,512]{1,0:T(8,128)} %constant.89.clone.refs_2_) | copy-start | bytes 393220
  10.9 26.4 %copy-start.6 = (f32[128,256]{1,0:T(8,128)S(1)}, f32[128,256]{1,0:T(8,128)}, u32[]{:S(2)}) copy-start(f32[128,256]{1,0:T(8,128)} %constant.92.clone.refs_5_) | copy-start | bytes 393220
  10.9 26.4 %copy-start.7 = (f32[128,256]{1,0:T(8,128)S(1)}, f32[128,256]{1,0:T(8,128)}, u32[]{:S(2)}) copy-start(f32[128,256]{1,0:T(8,128)} %constant.95.clone.refs_8_) | copy-start | bytes 393220
  11.0 26.4 %copy-start.10 = (f32[64,32]{1,0:T(8,128)S(1)}, f32[64,32]{1,0:T(8,128)}, u32[]{:S(2)}) copy-start(f32[64,32]{1,0:T(8,128)} %constant.91.clone.refs_4_) | copy-start | bytes 24580
  12.5 24.8 %copy-start.1 = (f32[256,512]{1,0:T(8,128)S(1)}, f32[256,512]{1,0:T(8,128)}, u32[]{:S(2)}) copy-start(f32[256,512]{1,0:T(8,128)} %constant.93.clone.refs_6_) | copy-start | bytes 1572868
  16.3 21.1 %copy-start.9 = (f32[64,128]{1,0:T(8,128)S(1)}, f32[64,128]{1,0:T(8,128)}, u32[]{:S(2)}) copy-start(f32[64,128]{1,0:T(8,128)} %constant.90.clone.refs_3_) | copy-start | bytes 98308
  16.3 21.0 %all-to-all-start = ((f32[32,1,2176]{2,1,0:T(1,128)}), f32[32,1,2176]{2,1,0:T(1,128)S(1)}, u32[]{:S(2)}, u32[]{:S(2)}) async-start(f32[32,1,2176]{2,1,0:T(1,128)} %bitcast.14), calls=%async_computation | async-start | bytes 557056 | tf_op jit(solution)/shard_map/all_to_all | solution.py:428
  25.0 12.4 %copy-start.8 = (f32[128,64]{1,0:T(8,128)S(1)}, f32[128,64]{1,0:T(8,128)}, u32[]{:S(2)}) copy-start(f32[128,64]{1,0:T(8,128)} %constant.96.clone.refs_9_) | copy-start | bytes 98308
  43.0 12.9 %all-to-all-start.2 = ((f32[8,40,128]{2,1,0:T(8,128)}), f32[8,40,128]{2,1,0:T(8,128)S(1)}, u32[]{:S(2)}, u32[]{:S(2)}) async-start(f32[8,40,128]{2,1,0:T(8,128)} %middle_part.1), calls=%async_computation.2 | async-start | bytes 327680 | tf_op jit(solution)/shard_map/all_to_all | solution.py:428
  56.6 17.2 %copy-start.4 = (f32[128,512]{1,0:T(8,128)S(1)}, f32[128,512]{1,0:T(8,128)}, u32[]{:S(2)}) copy-start(f32[128,512]{1,0:T(8,128)} %constant.100.clone.refs_4_) | copy-start | bytes 786436
  56.6 17.2 %all-to-all-start.3 = ((f32[8,40,128]{2,1,0:T(8,128)}), f32[8,40,128]{2,1,0:T(8,128)S(1)}, u32[]{:S(2)}, u32[]{:S(2)}) async-start(f32[8,40,128]{2,1,0:T(8,128)} %repeat_sum.1), calls=%async_computation.3 | async-start | bytes 327680 | tf_op jit(solution)/shard_map/all_to_all | solution.py:428
  65.7 8.1 %copy-start.14 = (f32[1,512]{1,0:T(1,128)S(1)}, f32[1,512]{1,0:T(1,128)}, u32[]{:S(2)}) copy-start(f32[1,512]{1,0:T(1,128)} %constant.101.clone.refs_5_) | copy-start | bytes 6148

commit v5 on v4

--- a/solution.py
+++ b/solution.py
@@ -196,14 +196,13 @@
     return (inside <= limit_value).astype(jnp.float32)
 
 
-def middle_math(
+def field_math(
     half,
     weight,
     row_shift,
     col_shift,
     main,
     edge,
-    target,
     turn,
     rows,
     inner,
@@ -211,9 +210,6 @@
     spread,
     to_samples,
     interpolate,
-    fold_columns,
-    fold_rows,
-    pick,
 ):
     both = dot(dot(rows, main), spread)
     inside = dot_nt(inner, edge)
@@ -258,6 +254,29 @@
     near = jnp.concatenate([samples] + [roll(samples, MC - STEP * j) for j in range(1, NEAR)], axis=0)
     intensity = dot(near, interpolate)
     resist = logistic(steepness * (intensity - threshold_level))
+    return field, resist
+
+
+def adjoint_math(
+    half,
+    weight,
+    row_shift,
+    col_shift,
+    target,
+    resist,
+    field,
+    turn,
+    to_samples,
+    interpolate,
+    fold_columns,
+    fold_rows,
+    pick,
+):
+    opened = [pupil(row_shift[s], col_shift[s]) for s in range(POINTS)]
+    total = 0.0
+    for s in range(POINTS):
+        total = total + weight[s]
+    share = 1.0 / jnp.full((ROWS, MC), total, jnp.float32)
     slope = (
         2.0
         * loss_weight
@@ -334,57 +353,108 @@
     return lax.dynamic_index_in_dim(jnp.asarray(table), index, 0, False)
 
 
-def columns_part(mask_param):
+def columns_part(row_index, mask_param, target):
     tables = (column_table(), *turn_tables(), fold_tables()[2])
+    turn = own_row_table()
     if not KERNELS:
-        return repeated(jnp.concatenate(columns_math(mask_param, *tables)), ROW_BLOCKS)
-
-    def kernel(mask_ref, *refs):
-        *refs, out_ref = refs
+        message = jnp.concatenate(columns_math(mask_param, *tables))
+        return repeated(message, ROW_BLOCKS), repeated(target, NEAR), pick_block(turn, row_index)
+
+    def kernel(place, mask_ref, target_ref, turn_ref, *refs):
+        *refs, out_ref, near_ref, own_ref = refs
+        own_ref[...] = turn_ref[0]
+        for b in range(NEAR):
+            near_ref[b] = target_ref[...]
         main, edge = columns_math(mask_ref[...], *[ref[...] for ref in refs])
         for b in range(ROW_BLOCKS):
             out_ref[LINES * b : LINES * b + ROWS] = main
             out_ref[LINES * b + ROWS : LINES * (b + 1)] = edge
 
-    sent = call(kernel, plain(ROW_BLOCKS * LINES, KC), "columns_part", (), (mask_param, *tables))
-    return sent.reshape(ROW_BLOCKS, 1, LINES * KC)
+    full = lambda shape: pl.BlockSpec(shape, lambda i, place: (0,) * len(shape))
+    outputs = (
+        plain(ROW_BLOCKS * LINES, KC),
+        jax.ShapeDtypeStruct((NEAR, *target.shape), target.dtype),
+        plain(*turn.shape[1:]),
+    )
+    sent, near, own = pl.pallas_call(
+        kernel,
+        grid_spec=pltpu.PrefetchScalarGridSpec(
+            num_scalar_prefetch=1,
+            grid=(1,),
+            in_specs=[
+                full(mask_param.shape),
+                full(target.shape),
+                pl.BlockSpec((1, *turn.shape[1:]), lambda i, place: (place[0], 0, 0)),
+                *[full(table.shape) for table in tables],
+            ],
+            out_specs=tuple(full(output.shape) for output in outputs),
+        ),
+        out_shape=outputs,
+        name="columns_part",
+    )(row_index.reshape(1), mask_param, target, turn, *tables)
+    return sent.reshape(ROW_BLOCKS, 1, LINES * KC), near, own
 
 
 def repeated(values, count):
     return jnp.broadcast_to(values[None], (count, *values.shape))
 
 
-def middle_part(half, weight, row_shift, col_shift, heard, target, turn):
+def field_part(half, weight, row_shift, col_shift, heard, turn):
     heard = heard.reshape(ROW_BLOCKS * LINES, KC)
     arrays = (
         heard,
-        target.reshape(NEAR * ROWS, SHARE),
         turn,
         *band_tables(),
         spread_table(),
         f32(sample_table()),
         f32(interpolation_table()),
-        *fold_tables(),
     )
     scalars = (half.reshape(1), weight, row_shift, col_shift)
     if not KERNELS:
         lines = heard.reshape(ROW_BLOCKS, LINES, KC)
         main, edge = lines[:, :ROWS].reshape(NR, KC), lines[:, ROWS]
-        return repeated(middle_math(half, *scalars[1:], main, edge, *arrays[1:]), 8)
+        return field_math(half, *scalars[1:], main, edge, *arrays[1:])
 
     def kernel(half_ref, weight_ref, row_ref, col_ref, heard_ref, *refs):
-        *refs, out_ref = refs
+        *refs, field_ref, resist_ref = refs
         main = jnp.concatenate(
             [heard_ref[LINES * b : LINES * b + ROWS] for b in range(ROW_BLOCKS)], axis=0
         )
         edge = heard_ref[pl.ds(ROWS, ROW_BLOCKS, stride=LINES)]
-        message = middle_math(
+        field_ref[...], resist_ref[...] = field_math(
             half_ref[0], weight_ref, row_ref, col_ref, main, edge, *[ref[...] for ref in refs]
+        )
+
+    outputs = (
+        pltpu.VMEM((POINTS * ROWS, 2 * MC), jnp.float32),
+        pltpu.VMEM((NEAR * ROWS, SHARE), jnp.float32),
+    )
+    return call(kernel, outputs, "field_part", scalars, arrays)
+
+
+def adjoint_part(half, weight, row_shift, col_shift, target, resist, field, turn):
+    arrays = (
+        target.reshape(NEAR * ROWS, SHARE),
+        resist,
+        field,
+        turn,
+        f32(sample_table()),
+        f32(interpolation_table()),
+        *fold_tables(),
+    )
+    scalars = (half.reshape(1), weight, row_shift, col_shift)
+    if not KERNELS:
+        return repeated(adjoint_math(half, *scalars[1:], *arrays), 8)
+
+    def kernel(half_ref, weight_ref, row_ref, col_ref, *refs):
+        *refs, out_ref = refs
+        message = adjoint_math(
+            half_ref[0], weight_ref, row_ref, col_ref, *[ref[...] for ref in refs]
         )
         for b in range(8):
             out_ref[b] = message
 
-    return call(kernel, plain(8, 40, KC), "middle_part", scalars, arrays)
+    return call(kernel, plain(8, 40, KC), "adjoint_part", scalars, arrays)
 
 
 def repeat_sum(received):
@@ -433,10 +503,12 @@
     src_index = lax.axis_index(("zh", "x", "c"))
     row_index = lax.axis_index(("zl", "y"))
     source = (source_weight, row_shift, col_shift)
-    turn = pick_block(own_row_table(), row_index)
-    near = swap(repeated(target, NEAR), ("x", "c"))
-    heard = swap(columns_part(mask_param), ("zl", "y"))
-    message = repeat_sum(swap(middle_part(half, *source, heard, near, turn), "y"))
+    sent, near, turn = columns_part(row_index, mask_param, target)
+    heard = swap(sent, ("zl", "y"))
+    near = swap(near, ("x", "c"))
+    field, resist = field_part(half, *source, heard, turn)
+    message = adjoint_part(half, *source, near, resist, field, turn)
+    message = repeat_sum(swap(message, "y"))
     return final_part(src_index, row_index, swap(message, ("zh", "zl")), mask_param)
 
 

time: 76.2 us -> 75.9 us (level)
  blocking collectives: 0 us -> 25.7 us
  waiting for transfers between devices: 32.8 us -> 19.4 us
  starting transfers between devices: 29.2 us -> 16.2 us
  Pallas kernels: 8.94 us -> 11 us
  local copies, waits for them, and re-layouts: 3.75 us -> 2.19 us
    all_to_all x0 -> x1, blocking collectives: none -> 25.7 us  [swap(): return lax.all_to_all(values, axis, 0, 0, tiled=True)]
    all_to_all x4 -> x3, waiting for transfers between devices: 32.8 us -> 19.4 us  [swap(): return lax.all_to_all(values, axis, 0, 0, tiled=True)]
    all_to_all x4 -> x3, starting transfers between devices: 29.2 us -> 16.2 us  [swap(): return lax.all_to_all(values, axis, 0, 0, tiled=True)]
    pallas_call x0 -> x1, Pallas kernels: none -> 2.76 us  [columns_part(): pl.pallas_call(kernel, grid_spec=pltpu.PrefetchScalarGridSpec(num_scalar_...]
    broadcast_in_dim x1 -> x0, local copies, waits for them, and re-layouts: 1.55 us -> none  [repeated(): return jnp.broadcast_to(values[None], (count, *values.shape))]
    squeeze x3 -> x2, local copies, waits for them, and re-layouts: 2.13 us -> 1.37 us  [pick_block(): return lax.dynamic_index_in_dim(jnp.asarray(table), index, 0, False)]
  transfers between devices with their start and end apart: 4 -> 3, of which waited for: 4 -> 3; matrix products, arithmetic and copies ran while one was open for 3% -> 3% of each run, Pallas kernels for 2% -> 4%
where the time goes in v5:
time: 75.9 us; the launch traced here: 74.5 us
  blocking collectives  25.7 us (34%)
  waiting for transfers between devices  19.4 us (26%)
  starting transfers between devices  16.2 us (21%)
  Pallas kernels  11 us (14%)
  local copies, waits for them, and re-layouts  2.19 us (3%)
    all_to_all x1, blocking collectives, swap(): return lax.all_to_all(values, axis, 0, 0, tiled=True)  25.7 us
    all_to_all x3, waiting for transfers between devices, swap(): return lax.all_to_all(values, axis, 0, 0, tiled=True)  19.4 us
    all_to_all x3, starting transfers between devices, swap(): return lax.all_to_all(values, axis, 0, 0, tiled=True)  16.2 us
    pallas_call x4, Pallas kernels, call(): pl.pallas_call(body, in_specs=[SMEM] * len(scalars) + [VMEM] * len(arrays...  8.23 us
    pallas_call x1, Pallas kernels, columns_part(): pl.pallas_call(kernel, grid_spec=pltpu.PrefetchScalarGridSpec(num_scalar_...  2.76 us
  transfers between devices with their start and end apart: 3, of which 3 were waited for; matrix products, arithmetic and copies ran while one was open for 3% of the time, Pallas kernels for 4%

profile of v5, /device:TPU:6, one launch (start us, length us, event | category | flops | bytes accessed | tf_op | source)
XLA Modules:
  0.0 74.5 jit_solution(10409089657822810084)
XLA Ops:
  0.0 0.0 copy-start.4
  0.0 0.0 copy-start.5
  0.0 0.0 copy-start.8
  0.0 0.0 copy-start.9
  0.0 2.8 %columns_part.1 = (f32[544,128]{1,0:T(8,128)}, s32[8,16,512]{2,1,0:T(8,128)}, f32[32,64]{1,0:T(8,128)}) custom-call(s32[1]{0:T(128)} %bitcast.1.place, f32[16,8192]{1,0:T(8,128)} %mask_ref.1, s32[16,512]{1,0:T(8,128)} %target_ref.1, f32[32,32,64]{2,1,0:T(8,128)} %constant.80.clone.turn_ref, f32[136,512]{1,0:T(8,128)} %constant.81.clone.refs_0_, ...), custom_call_target="tpu_custom_call" | custom-call | tf_op jit(solution)/shard_map/columns_part/pallas_call | solution.py:379
  2.8 0.0 copy-start
  2.8 0.0 copy-start.1
  2.8 25.7 %all_to_all.20 = f32[32,1,2176]{2,1,0:T(1,128)S(1)} all-to-all(f32[32,1,2176]{2,1,0:T(1,128)} %bitcast.13), channel_id=1, replica_groups=mesh['zh'=2,'x'=4,'c'=2,'zl'=4,'y'=8] {'zl','y'}, dimensions={0} | all-to-all | bytes 557056 | tf_op jit(solution)/shard_map/all_to_all | solution.py:498
  28.5 0.0 copy-start.6
  28.5 4.9 %all-to-all-start = ((s32[8,16,512]{2,1,0:T(8,128)}), s32[8,16,512]{2,1,0:T(8,128)S(1)}, u32[]{:S(2)}, u32[]{:S(2)}) async-start(s32[8,16,512]{2,1,0:T(8,128)} %get-tuple-element.10), calls=%async_computation | async-start | bytes 524288 | tf_op jit(solution)/shard_map/all_to_all | solution.py:498
  33.4 0.0 copy-done.4
  33.4 0.0 copy-done.5
  33.4 0.0 copy-done.8
  33.4 0.0 copy-done.9
  33.4 0.0 copy-done
  33.4 0.0 copy-done.1
  33.4 0.0 copy-done.6
  33.4 0.0 copy-start.3
  33.5 0.0 copy-start.7
  33.5 2.7 %field_part.1 = (f32[256,512]{1,0:T(8,128)S(1)}, f32[128,512]{1,0:T(8,128)S(1)}) custom-call(s32[1]{0:T(128)} %bitcast.half_ref, f32[16]{0:T(128)} %weight_ref.3, s32[16]{0:T(128)} %row_ref.3, s32[16]{0:T(128)} %col_ref.3, f32[544,128]{1,0:T(8,128)S(1)} %bitcast.11, f32[32,64]{1,0:T(8,128)S(1)} %copy-done.6, f32[64,512]{1,0:T(8,128)S(1)} %copy-done.4, ...), custom_call_target="tpu_custom_call" | custom-call | tf_op jit(solution)/shard_map/field_part/pallas_call | solution.py:339
  36.1 0.0 copy-start.10
  36.2 2.7 %all-to-all-done = s32[8,16,512]{2,1,0:T(8,128)S(1)} async-done(((s32[8,16,512]{2,1,0:T(8,128)}), s32[8,16,512]{2,1,0:T(8,128)S(1)}, u32[]{:S(2)}, u32[]{:S(2)}) %all-to-all-start) | async-done | bytes 262176 | tf_op jit(solution)/shard_map/all_to_all | solution.py:498
  38.8 0.0 copy-done.3
  38.8 0.0 copy-done.7
  38.8 0.0 copy-done.10
  38.8 3.8 %adjoint_part.1 = f32[8,40,128]{2,1,0:T(8,128)} custom-call(s32[1]{0:T(128)} %bitcast.half_ref, f32[16]{0:T(128)} %weight_ref.3, s32[16]{0:T(128)} %row_ref.3, s32[16]{0:T(128)} %col_ref.3, s32[128,512]{1,0:T(8,128)S(1)} %bitcast.12, f32[128,512]{1,0:T(8,128)S(1)} %get-tuple-element.13.refs_1_, f32[256,512]{1,0:T(8,128)S(1)} %get-tuple-element.14.refs_2_, ...), custom_call_target="tpu_custom_call" | custom-call | tf_op jit(solution)/shard_map/adjoint_part/pallas_call | solution.py:339
  42.6 3.6 %all-to-all-start.2 = ((f32[8,40,128]{2,1,0:T(8,128)}), f32[8,40,128]{2,1,0:T(8,128)S(1)}, u32[]{:S(2)}, u32[]{:S(2)}) async-start(f32[8,40,128]{2,1,0:T(8,128)} %adjoint_part.1), calls=%async_computation.2 | async-start | bytes 327680 | tf_op jit(solution)/shard_map/all_to_all | solution.py:498
  46.2 9.4 %all-to-all-done.2.in_ref = f32[8,40,128]{2,1,0:T(8,128)S(1)} async-done(((f32[8,40,128]{2,1,0:T(8,128)}), f32[8,40,128]{2,1,0:T(8,128)S(1)}, u32[]{:S(2)}, u32[]{:S(2)}) %all-to-all-start.2) | async-done | bytes 163872 | tf_op jit(solution)/shard_map/all_to_all | solution.py:498
  55.6 0.7 repeat_sum.1
  56.3 0.0 copy-start.2
  56.3 7.7 %all-to-all-start.3 = ((f32[8,40,128]{2,1,0:T(8,128)}), f32[8,40,128]{2,1,0:T(8,128)S(1)}, u32[]{:S(2)}, u32[]{:S(2)}) async-start(f32[8,40,128]{2,1,0:T(8,128)} %repeat_sum.1), calls=%async_computation.3 | async-start | bytes 327680 | tf_op jit(solution)/shard_map/all_to_all | solution.py:498
  64.0 0.7 fusion
  64.7 0.7 dynamic-slice_bitcast_fusion.refs_1_
  65.4 0.8 %constant_dynamic-slice_fusion.2.refs_0_ = f32[16,512]{1,0:T(8,128)S(1)} fusion(f32[16,8192]{1,0:T(8,128)} %mask_ref.1, s32[]{:T(128)S(6)} %select_n.12), kind=kLoop, calls=%fused_computation.3 | loop fusion | bytes 65540 | tf_op jit(solution)/shard_map/dynamic_slice | solution.py:478
  66.2 0.0 copy-start.11
  66.2 7.3 %all-to-all-done.3.in_ref = f32[8,40,128]{2,1,0:T(8,128)S(1)} async-done(((f32[8,40,128]{2,1,0:T(8,128)}), f32[8,40,128]{2,1,0:T(8,128)S(1)}, u32[]{:S(2)}, u32[]{:S(2)}) %all-to-all-start.3) | async-done | bytes 163872 | tf_op jit(solution)/shard_map/all_to_all | solution.py:498
  73.5 0.0 copy-done.2
  73.5 0.0 copy-done.11
  73.5 1.1 %final_part.1 = f32[16,512]{1,0:T(8,128)} custom-call(f32[8,40,128]{2,1,0:T(8,128)S(1)} %all-to-all-done.3.in_ref, f32[16,512]{1,0:T(8,128)S(1)} %constant_dynamic-slice_fusion.2.refs_0_, f32[16,128]{1,0:T(8,128)S(1)} %dynamic-slice_bitcast_fusion.refs_1_, f32[1,128]{1,0:T(1,128)S(1)} %get-tuple-element.15.refs_2_, f32[1,128]{1,0:T(1,128)S(1)} %get-tuple-element.16.refs_3_, ...), custom_call_target="tpu_custom_call" | custom-call | tf_op jit(solution)/shard_map/final_part/pallas_call | solution.py:339
Async XLA Ops:
  0.0 33.4 %copy-start.4 = (f32[64,512]{1,0:T(8,128)S(1)}, f32[64,512]{1,0:T(8,128)}, u32[]{:S(2)}) copy-start(f32[64,512]{1,0:T(8,128)} %constant.85.clone.refs_1_) | copy-start | bytes 393220
  0.0 33.4 %copy-start.5 = (f32[128,256]{1,0:T(8,128)S(1)}, f32[128,256]{1,0:T(8,128)}, u32[]{:S(2)}) copy-start(f32[128,256]{1,0:T(8,128)} %constant.88.clone.refs_4_) | copy-start | bytes 393220
  0.0 33.4 %copy-start.8 = (f32[64,128]{1,0:T(8,128)S(1)}, f32[64,128]{1,0:T(8,128)}, u32[]{:S(2)}) copy-start(f32[64,128]{1,0:T(8,128)} %constant.86.clone.refs_2_) | copy-start | bytes 98308
  0.0 33.4 %copy-start.9 = (f32[64,32]{1,0:T(8,128)S(1)}, f32[64,32]{1,0:T(8,128)}, u32[]{:S(2)}) copy-start(f32[64,32]{1,0:T(8,128)} %constant.87.clone.refs_3_) | copy-start | bytes 24580
  2.8 30.6 %copy-start = (f32[256,512]{1,0:T(8,128)S(1)}, f32[256,512]{1,0:T(8,128)}, u32[]{:S(2)}) copy-start(f32[256,512]{1,0:T(8,128)} %constant.89.clone.refs_5_.refs_4_) | copy-start | bytes 1572868
  2.8 30.6 %copy-start.1 = (f32[256,512]{1,0:T(8,128)S(1)}, f32[256,512]{1,0:T(8,128)}, u32[]{:S(2)}) copy-start(f32[256,512]{1,0:T(8,128)} %constant.90.clone.refs_6_.refs_5_) | copy-start | bytes 1572868
  28.5 5.0 %copy-start.6 = (f32[32,64]{1,0:T(8,128)S(1)}, f32[32,64]{1,0:T(8,128)}, u32[]{:S(2)}) copy-start(f32[32,64]{1,0:T(8,128)} %get-tuple-element.12.refs_0_.refs_3_) | copy-start | bytes 24580
  28.5 10.3 %all-to-all-start = ((s32[8,16,512]{2,1,0:T(8,128)}), s32[8,16,512]{2,1,0:T(8,128)S(1)}, u32[]{:S(2)}, u32[]{:S(2)}) async-start(s32[8,16,512]{2,1,0:T(8,128)} %get-tuple-element.10), calls=%async_computation | async-start | bytes 524288 | tf_op jit(solution)/shard_map/all_to_all | solution.py:498
  33.4 5.4 %copy-start.3 = (f32[128,256]{1,0:T(8,128)S(1)}, f32[128,256]{1,0:T(8,128)}, u32[]{:S(2)}) copy-start(f32[128,256]{1,0:T(8,128)} %constant.91.clone.refs_6_) | copy-start | bytes 393220
  33.5 5.4 %copy-start.7 = (f32[128,64]{1,0:T(8,128)S(1)}, f32[128,64]{1,0:T(8,128)}, u32[]{:S(2)}) copy-start(f32[128,64]{1,0:T(8,128)} %constant.92.clone.refs_7_) | copy-start | bytes 98308
  36.1 2.7 %copy-start.10 = (f32[8,128]{1,0:T(8,128)S(1)}, f32[8,128]{1,0:T(8,128)}, u32[]{:S(2)}) copy-start(f32[8,128]{1,0:T(8,128)} %constant.84.clone.refs_3_.refs_8_) | copy-start | bytes 12292
  42.6 13.0 %all-to-all-start.2 = ((f32[8,40,128]{2,1,0:T(8,128)}), f32[8,40,128]{2,1,0:T(8,128)S(1)}, u32[]{:S(2)}, u32[]{:S(2)}) async-start(f32[8,40,128]{2,1,0:T(8,128)} %adjoint_part.1), calls=%async_computation.2 | async-start | bytes 327680 | tf_op jit(solution)/shard_map/all_to_all | solution.py:498
  56.3 17.2 %copy-start.2 = (f32[128,512]{1,0:T(8,128)S(1)}, f32[128,512]{1,0:T(8,128)}, u32[]{:S(2)}) copy-start(f32[128,512]{1,0:T(8,128)} %constant.96.clone.refs_4_) | copy-start | bytes 786436
  56.3 17.1 %all-to-all-start.3 = ((f32[8,40,128]{2,1,0:T(8,128)}), f32[8,40,128]{2,1,0:T(8,128)S(1)}, u32[]{:S(2)}, u32[]{:S(2)}) async-start(f32[8,40,128]{2,1,0:T(8,128)} %repeat_sum.1), calls=%async_computation.3 | async-start | bytes 327680 | tf_op jit(solution)/shard_map/all_to_all | solution.py:498
  66.2 7.3 %copy-start.11 = (f32[1,512]{1,0:T(1,128)S(1)}, f32[1,512]{1,0:T(1,128)}, u32[]{:S(2)}) copy-start(f32[1,512]{1,0:T(1,128)} %constant.97.clone.refs_5_) | copy-start | bytes 6148
